TPU v7x, 32 devices: a whole 2x2x4 slice. The times are simulated.
32 devices in a mesh: sample: 2 (over x), space: 16 (over z, y, core).
Axes of the slice: x: 2, y: 2, z: 4, core: 2. Of those that a mesh axis runs over, the one named last changes fastest.
Arguments:
- features: bfloat16 [2, 4, 128, 128, 128], P('sample', None, 'space'), parts along dimension 0, may hold values from -6 to 6
- log_perm: float32 [2, 128, 128, 128], P('sample', 'space'), parts along dimension 0, may hold values from -1.5 to 1.5
- well_cells: int32 [2, 32], P('sample'), parts along dimension 0, may hold values from 0 to 2097151
- well_rates: float32 [2, 32], P('sample'), parts along dimension 0, may hold values from 10 to 70
- lift_in: bfloat16 [5, 128], replicated, may hold values from -2.5 to 2.5
- lift_out: bfloat16 [128, 32], replicated, may hold values from -0.5 to 0.5
- spec_weight: bfloat16 [2, 1024, 32, 2048], P(None, 'space'), may hold values from -2 to 2
- point_weight: bfloat16 [2, 32, 32], replicated, may hold values from -1 to 1
- dec_in: bfloat16 [32, 64], replicated, may hold values from -1 to 1
- dec_out: bfloat16 [64, 2], replicated, may hold values from -0.75 to 0.75
Outputs:
- states: float32 [2, 2, 128, 128, 128], P('sample', None, 'space'), parts along dimension 0
- residual: float32 [2, 128, 128, 128], P('sample', 'space'), parts along dimension 0
There are 2 independent parts, one for each index of `sample`. A program takes and returns all parts, laid end to end along the dimension named above; an argument that names none is the same for every part. Nothing has to cross between parts.
Inputs may be any that keep to these rules, and one draw needn't show every extreme that they name: `well_cells`: cells of the sample's grid; several wells may share a cell.
All inputs are finite; a program needn't handle non-finite values.
Results may differ from a plain program's by a relative error of at most 0.03.
Values may be sent and summed in bfloat16 or wider, within the bound.
A program may use at most 192 MiB of HBM per device.

v0:
```python
import math

import jax
import jax.numpy as jnp
import numpy as np
from jax import lax
from jax.experimental import pallas as pl
from jax.experimental.pallas import tpu as pltpu
from jax.sharding import PartitionSpec as P

NX = 128
NY = 128
NZ = 128
MX = 32
MY = 32
MZ = 32
C = 32
FIN = 4
LAYERS = 2
WELLS = 32


def padded_2(block, sides, width):
    for axis, dim in sides:
        count = lax.axis_size(axis)
        forward = [(i, i + 1) for i in range(count - 1)]
        backward = [(target, source) for source, target in forward]
        low = lax.ppermute(
            lax.slice_in_dim(block, block.shape[dim] - width, None, axis=dim), axis, forward
        )
        high = lax.ppermute(lax.slice_in_dim(block, 0, width, axis=dim), axis, backward)
        block = jnp.concatenate([low, block, high], axis=dim)
    return block


def freq_table(length, kept, one_sided):
    indices = jnp.arange(kept, dtype=jnp.int32)
    if one_sided:
        return indices
    return jnp.where(indices < kept // 2, indices, length - kept + indices)


def wave_parts(length, kept, one_sided):
    freqs = freq_table(length, kept, one_sided)
    places = jnp.arange(length, dtype=jnp.int32)
    phase_turns = freqs[:, None] * places[None, :] % length
    angles = phase_turns.astype(jnp.float32) * (2.0 * math.pi / length)
    norm_scale = 1.0 / math.sqrt(length)
    return (jnp.cos(angles) * norm_scale, jnp.sin(angles) * norm_scale)


def forward_table(length, kept):
    cosine_vals, sine_vals = wave_parts(length, kept, False)
    return jnp.stack(
        [jnp.stack([cosine_vals.T, -sine_vals.T], 1), jnp.stack([sine_vals.T, cosine_vals.T], 1)], 1
    ).astype(jnp.bfloat16)


def inverse_table(length, kept):
    cosine_vals, sine_vals = wave_parts(length, kept, False)
    return jnp.stack(
        [jnp.stack([cosine_vals, sine_vals], 1), jnp.stack([-sine_vals, cosine_vals], 1)], 1
    ).astype(jnp.bfloat16)


def z_tables():
    cosine_vals, sine_vals = wave_parts(NZ, MZ, True)
    weights_k = jnp.where(jnp.arange(MZ) == 0, 1.0, 2.0).astype(jnp.float32)[:, None]
    z_forward = jnp.concatenate([cosine_vals.T, -sine_vals.T], 1).astype(jnp.bfloat16)
    z_inverse = jnp.concatenate([weights_k * cosine_vals, -weights_k * sine_vals], 0).astype(
        jnp.bfloat16
    )
    return (z_forward, z_inverse)


def gelu_tanh(values):
    return jax.nn.gelu(values, approximate=True)


def face_term(cond_a, cond_b, press_a, press_b):
    return 2.0 * cond_a * cond_b / (cond_a + cond_b) * (press_a - press_b)


def mobility_of(saturation, log_values):
    return jnp.exp(log_values) * (
        saturation * saturation + 0.5 * (1.0 - saturation) * (1.0 - saturation)
    )


def darcy(pressure, conduct, well_cells, well_rates):
    batches, planes = pressure.shape[0], pressure.shape[1]
    space_index = lax.axis_index("space")
    pad_cond = jnp.pad(conduct, ((0, 0), (0, 0), (1, 1), (1, 1)))
    pad_press = jnp.pad(pressure, ((0, 0), (0, 0), (1, 1), (1, 1)))
    flux_sum = face_term(conduct, pad_cond[:, :, 2:, 1:-1], pressure, pad_press[:, :, 2:, 1:-1])
    flux_sum = flux_sum + face_term(
        conduct, pad_cond[:, :, :-2, 1:-1], pressure, pad_press[:, :, :-2, 1:-1]
    )
    flux_sum = flux_sum + face_term(
        conduct, pad_cond[:, :, 1:-1, 2:], pressure, pad_press[:, :, 1:-1, 2:]
    )
    flux_sum = flux_sum + face_term(
        conduct, pad_cond[:, :, 1:-1, :-2], pressure, pad_press[:, :, 1:-1, :-2]
    )
    fields = jnp.stack([pressure, conduct], 1)
    padded = padded_2(fields.astype(jnp.bfloat16), (("space", 2),), 1).astype(fields.dtype)
    press_low = padded[:, 0, 0]
    press_high = padded[:, 0, -1]
    cond_low = padded[:, 1, 0]
    cond_high = padded[:, 1, -1]
    press_below = jnp.concatenate([press_low[:, None], pressure[:, :-1]], 1)
    cond_below = jnp.concatenate([cond_low[:, None], conduct[:, :-1]], 1)
    press_above = jnp.concatenate([pressure[:, 1:], press_high[:, None]], 1)
    cond_above = jnp.concatenate([conduct[:, 1:], cond_high[:, None]], 1)
    lower_terms = face_term(conduct, cond_below, pressure, press_below)
    upper_terms = face_term(conduct, cond_above, pressure, press_above)
    flux_sum = flux_sum + lower_terms + upper_terms
    well_x = well_cells // (NY * NZ) - space_index * planes
    well_y = well_cells // NZ % NY
    well_z = well_cells % NZ
    onehot_x = (well_x[:, :, None] == jnp.arange(planes, dtype=jnp.int32)[None, None, :]).astype(
        jnp.float32
    ) * well_rates[:, :, None]
    onehot_y = (well_y[:, :, None] == jnp.arange(NY, dtype=jnp.int32)[None, None, :]).astype(
        jnp.float32
    )
    onehot_z = (well_z[:, :, None] == jnp.arange(NZ, dtype=jnp.int32)[None, None, :]).astype(
        jnp.float32
    )
    plane_rows = (onehot_x[:, :, :, None] * onehot_y[:, :, None, :]).reshape(
        batches, WELLS, planes * NY
    )
    source = jnp.einsum(
        "bwa,bwz->baz", plane_rows, onehot_z, precision=lax.Precision.HIGHEST
    ).reshape(batches, planes, NY, NZ)
    return flux_sum - source


def local_general(
    features,
    log_perm,
    well_cells,
    well_rates,
    lift_in,
    lift_out,
    spec_weight,
    point_weight,
    dec_in,
    dec_out,
):
    batches = features.shape[0]
    planes = features.shape[2]
    space_index = lax.axis_index("space")
    block = spec_weight.shape[1]
    cell_count = planes * NY * NZ
    z_forward, z_inverse = z_tables()
    y_forward = forward_table(NY, MY)
    y_inverse = inverse_table(NY, MY)
    x_forward = forward_table(NX, MX)
    x_inverse = inverse_table(NX, MX)
    perm_b = log_perm.astype(jnp.bfloat16).reshape(batches, 1, cell_count)
    lift_input = jnp.concatenate([features.reshape(batches, FIN, cell_count), perm_b], 1)
    lift_hidden = jnp.einsum("bfn,fh->bhn", lift_input, lift_in, preferred_element_type=jnp.float32)
    lifted = gelu_tanh(lift_hidden).astype(jnp.bfloat16)
    hidden_state = jnp.einsum(
        "bhn,hc->bcn", lifted, lift_out, preferred_element_type=jnp.float32
    ).astype(jnp.bfloat16)
    for layer_idx in range(LAYERS):
        zspec = jnp.dot(hidden_state.reshape(-1, NZ), z_forward, preferred_element_type=jnp.float32)
        zspec = zspec.astype(jnp.bfloat16).reshape(batches * C * planes, NY, 2, MZ)
        yz_spec = jnp.einsum(
            "aypk,ypqj->aqjk", zspec, y_forward, preferred_element_type=jnp.float32
        )
        yz_spec = yz_spec.astype(jnp.bfloat16).reshape(batches, C, planes, 2, MY * MZ)
        mode_weights = spec_weight[layer_idx].reshape(block, C, MX, 2, C)
        spectrum = jnp.einsum(
            "bcxpm,xpqi->bcqim",
            lax.all_to_all(yz_spec, "space", split_axis=4, concat_axis=2, tiled=True),
            x_forward,
            preferred_element_type=jnp.float32,
        ).astype(jnp.bfloat16)
        products = jnp.einsum(
            "bcqim,mcipo->bimqpo", spectrum, mode_weights, preferred_element_type=jnp.float32
        )
        real_part = products[:, :, :, 0, 0] - products[:, :, :, 1, 1]
        imag_part = products[:, :, :, 0, 1] + products[:, :, :, 1, 0]
        mixed_modes = jnp.stack([real_part, imag_part], 3).astype(jnp.bfloat16)
        back_field = jnp.einsum(
            "bimqo,iqpx->boxpm", mixed_modes, x_inverse, preferred_element_type=jnp.float32
        ).astype(jnp.bfloat16)
        returned = lax.all_to_all(back_field, "space", split_axis=2, concat_axis=4, tiled=True)
        returned = returned.reshape(batches * C * planes, 2, MY, MZ)
        y_back = jnp.einsum(
            "aqjk,jqpy->aypk", returned, y_inverse, preferred_element_type=jnp.float32
        ).astype(jnp.bfloat16)
        spectral = jnp.dot(
            y_back.reshape(-1, 2 * MZ), z_inverse, preferred_element_type=jnp.float32
        ).reshape(batches, C, cell_count)
        local_term = jnp.einsum(
            "bcn,co->bon", hidden_state, point_weight[layer_idx], preferred_element_type=jnp.float32
        )
        hidden_state = gelu_tanh(spectral + local_term).astype(jnp.bfloat16)
    decoded = gelu_tanh(
        jnp.einsum("bcn,cd->bdn", hidden_state, dec_in, preferred_element_type=jnp.float32)
    ).astype(jnp.bfloat16)
    decoded_out = jnp.einsum("bdn,de->ben", decoded, dec_out, preferred_element_type=jnp.float32)
    pressure = decoded_out[:, 0].reshape(batches, planes, NY, NZ)
    saturation = jax.nn.sigmoid(decoded_out[:, 1]).reshape(batches, planes, NY, NZ)
    states = jnp.stack([pressure, saturation], 1)
    conduct = mobility_of(saturation, log_perm)
    return (states, darcy(pressure, conduct, well_cells, well_rates))


BF = jnp.bfloat16
F32 = jnp.float32
PAIRS = NY // 2
PITCH = PAIRS + 8
MODE_STEP = 8
ROWS = 8
UNROLL = 4
LANES = 128


def np_waves(length, kept, one_sided):
    index = np.arange(kept)
    freqs = index if one_sided else np.where(index < kept // 2, index, length - kept + index)
    angles = (freqs[:, None] * np.arange(length)[None, :] % length) * (2.0 * math.pi / length)
    norm = 1.0 / math.sqrt(length)
    return np.cos(angles) * norm, np.sin(angles) * norm


def np_forward(length, kept):
    cosine, sine = np_waves(length, kept, False)
    return np.stack([np.stack([cosine.T, -sine.T], 1), np.stack([sine.T, cosine.T], 1)], 1)


def np_inverse(length, kept):
    cosine, sine = np_waves(length, kept, False)
    return np.stack([np.stack([cosine, sine], 1), np.stack([-sine, cosine], 1)], 1)


def by_plane(table, axis, count):
    planes = NX // count
    order = np.arange(NX).reshape(count, planes).T.reshape(-1)
    return np.take(table, order, axis)


def tables_for(count):
    own = MY // count
    cosine, sine = np_waves(NZ, MZ, True)
    twice = np.where(np.arange(MZ) == 0, 1.0, 2.0)[:, None]
    z_forward = np.concatenate([cosine.T, -sine.T], 1)
    z_inverse = np.concatenate([twice * cosine, -twice * sine], 0)
    y_forward = np_forward(NY, MY).reshape(PAIRS, 2, 2, 2, count, own)
    y_inverse = np_inverse(NY, MY).reshape(count, own, 2, 2, PAIRS, 2)
    pair = np.eye(2)
    tables = {
        "zf": np.kron(pair, z_forward),
        "zi": 0.5 * np.kron(pair, z_inverse),
        "yf": y_forward.transpose(3, 5, 4, 1, 2, 0).reshape(2 * MY, 2 * NY),
        "yi": y_inverse.transpose(5, 3, 4, 2, 1, 0).reshape(2 * NY, 2 * MY),
        "xf": by_plane(np_forward(NX, MX).transpose(1, 2, 3, 0).reshape(2, 2 * MX, NX), 2, count),
        "xi": by_plane(np_inverse(NX, MX).transpose(2, 3, 0, 1).reshape(2, NX, 2 * MX), 1, count),
    }
    return {name: jnp.asarray(table.astype(np.float32)).astype(BF) for name, table in tables.items()}


def dot32(a, b):
    return jnp.dot(a, b, preferred_element_type=F32)


def gelu_of_half(values):
    u = values.astype(BF)
    scale = math.sqrt(2.0 / math.pi)
    inner = u * (BF(2.0 * scale) + BF(8.0 * scale * 0.044715) * (u * u))
    return u + u * jnp.tanh(inner)


def swap_blocks(four):
    shape = four[0].shape
    lane = lax.broadcasted_iota(jnp.int32, shape, 1)
    low = lane < 64
    even = lane % 64 < 32
    a0, a1, a2, a3 = four

    def cross(a, b, keep, shift):
        return (
            jnp.where(keep, a, pltpu.roll(b, shift, 1)),
            jnp.where(keep, pltpu.roll(a, LANES - shift, 1), b),
        )

    b0, b2 = cross(a0, a2, low, 64)
    b1, b3 = cross(a1, a3, low, 64)
    c0, c1 = cross(b0, b1, even, 32)
    c2, c3 = cross(b2, b3, even, 32)
    return c0, c1, c2, c3


def send_plane(me, count, plane, send, recv, send_sem, recv_sem):
    for shift in range(1, count):
        target = lax.rem(me + shift, count)
        pltpu.make_async_remote_copy(
            src_ref=send.at[plane, target],
            dst_ref=recv.at[plane, me],
            send_sem=send_sem.at[plane],
            recv_sem=recv_sem.at[plane],
            device_id={"space": target},
            device_id_type=pl.DeviceIdType.MESH,
        ).start()
    recv[plane, me] = send[plane, me]


def wait_plane(count, plane, buffer, sem):
    part = buffer.at[plane, pl.ds(0, count - 1)]
    pltpu.make_async_copy(part, part, sem.at[plane]).wait()


def to_modes(plane, count, yf_ref, zs, flat, send):
    pieces = []
    for group in range(C // 4):
        four = [zs[(group * 4 + r) * PITCH : (group * 4 + r) * PITCH + PAIRS, :] for r in range(4)]
        pieces.append(jnp.concatenate([p.astype(BF) for p in swap_blocks(four)], 0))
    modes = dot32(yf_ref[...], jnp.concatenate(pieces, 1))
    tiles = C * MZ // LANES
    slots = 2 * MY // count * tiles
    for s in range(2 * MY // count):
        for t in range(tiles):
            flat[pl.ds(s * tiles + t, count, stride=slots), :] = modes[
                s * count : (s + 1) * count, t * LANES : (t + 1) * LANES
            ]
    send[plane] = flat[: count * slots, :].reshape(count, slots, LANES).astype(BF)


def lay_out(zs, start, values):
    for r in range(ROWS):
        zs[pl.ds(start + r, C, stride=PITCH), :] = values[r * C : (r + 1) * C, :]


def hid_rows(index):
    return pl.ds(pl.multiple_of(index * ROWS * C, ROWS * C), ROWS * C)


def lift_plane(plane, feat_ref, perm_ref, in_ref, lo_ref, zf_ref, hid, plain, xs, zs):
    for f in range(FIN + 1):
        plain[...] = perm_ref[0, plane] if f == FIN else feat_ref[0, f, plane].astype(F32)
        for y2 in range(2):
            xs[y2, pl.ds(f, PAIRS, stride=8), :] = plain[pl.ds(y2, PAIRS, stride=2), :]
    width = lo_ref.shape[1]

    def block(index, carry):
        start = pl.multiple_of(index * ROWS * 8, ROWS * 8)
        x = jnp.concatenate([xs[0, pl.ds(start, ROWS * 8), :], xs[1, pl.ds(start, ROWS * 8), :]], 1)
        lifted = gelu_of_half(dot32(in_ref[...], x.astype(BF)))
        parts = [
            dot32(lo_ref[...], lifted[r * width : (r + 1) * width, :]).astype(BF)
            for r in range(lifted.shape[0] // width)
        ]
        hidden = jnp.concatenate(parts, 0)
        hid[plane, hid_rows(index), :] = hidden
        lay_out(zs, index * ROWS, dot32(hidden, zf_ref[...]))
        return carry

    lax.fori_loop(0, PAIRS // ROWS, block, 0, unroll=UNROLL)


def from_modes(plane, count, recv, yi_ref, flat, zs):
    tiles = C * MZ // LANES
    slots = 2 * MY // count * tiles
    flat[: count * slots, :] = recv[plane].astype(F32).reshape(count * slots, LANES)
    rows = []
    for s in range(2 * MY // count):
        rows.append(
            jnp.concatenate(
                [flat[pl.ds(s * tiles + t, count, stride=slots), :] for t in range(tiles)], 1
            ).astype(BF)
        )
    back = dot32(yi_ref[...], jnp.concatenate(rows, 0))
    for group in range(C // 4):
        lanes = slice(group * LANES, (group + 1) * LANES)
        four = [back[g * PAIRS : (g + 1) * PAIRS, lanes] for g in range(4)]
        for r, piece in enumerate(swap_blocks(four)):
            zs[(group * 4 + r) * PITCH : (group * 4 + r) * PITCH + PAIRS, :] = piece


def layer_rows(plane, index, zs, hid, zi_ref, kp):
    start = index * ROWS
    parts = [zs[pl.ds(start + r, C, stride=PITCH), :].astype(BF) for r in range(ROWS)]
    spectral = dot32(jnp.concatenate(parts, 0), zi_ref[...])
    return gelu_of_half(spectral + dot32(kp, hid[plane, hid_rows(index), :]))


def middle_plane(plane, kp, zi_ref, zf_ref, hid, zs, zs2):
    def block(index, carry):
        hidden = layer_rows(plane, index, zs, hid, zi_ref, kp)
        hid[plane, hid_rows(index), :] = hidden
        lay_out(zs2, index * ROWS, dot32(hidden, zf_ref[...]))
        return carry

    lax.fori_loop(0, PAIRS // ROWS, block, 0, unroll=UNROLL)


def final_plane(plane, kp, zi_ref, di_ref, do_ref, perm_ref, hid, zs, st_ref, cond_ref):
    def block(index, carry):
        hidden = layer_rows(plane, index, zs, hid, zi_ref, kp)
        both = dot32(do_ref[...], gelu_of_half(dot32(di_ref[...], hidden)))
        for y2 in range(2):
            lanes = slice(y2 * NZ, (y2 + 1) * NZ)
            where = pl.ds(index * ROWS * 2 + y2, ROWS, stride=2)
            st_ref[0, 0, plane, where, :] = both[:ROWS, lanes]
            st_ref[0, 1, plane, where, :] = both[ROWS:, lanes]
        return carry

    lax.fori_loop(0, PAIRS // ROWS, block, 0, unroll=UNROLL)
    sat = jax.nn.sigmoid(st_ref[0, 1, plane])
    st_ref[0, 1, plane] = sat
    cond_ref[0, plane] = mobility_of(sat, perm_ref[0, plane])


def mix_modes(planes, count, recv, send, wbuf, xf_ref, xi_ref, flat, spec, mixed, turned, rhs):
    own = MY // count
    tiles = C * MZ // LANES
    slots = 2 * own * tiles
    every = count * planes
    wide = MX * 2 * C
    for plane in range(planes):
        flat[plane * count * slots : (plane + 1) * count * slots, :] = (
            recv[plane].astype(F32).reshape(count * slots, LANES)
        )
    total = 0.0
    for p in range(2):
        right = jnp.concatenate(
            [
                flat[pl.ds(p * own * tiles + t, every, stride=slots), :].astype(BF)
                for t in range(own * tiles)
            ],
            1,
        )
        total = total + dot32(xf_ref[p], right)
    spec[:, : 2 * MX] = total.T
    chunk = 512

    def step(index, carry):
        first = pl.multiple_of(index * MODE_STEP, MODE_STEP)
        base = first // MZ * (C * MZ) + first % MZ
        rows = [spec[pl.ds(base + r, C, stride=MZ), :] for r in range(MODE_STEP)]
        values = jnp.concatenate(rows, 0)[:, : 2 * MX].astype(BF)
        for piece in range(wide // chunk):
            lo = piece * chunk
            row = lax.broadcasted_iota(jnp.int32, (2 * MX, chunk), 0)
            col = lax.broadcasted_iota(jnp.int32, (2 * MX, chunk), 1) + lo
            weights = wbuf[pl.ds(first, MODE_STEP), :, lo : lo + chunk]
            weights = weights.reshape(MODE_STEP * C, chunk).astype(F32)
            sums = []
            for q in range(2):
                pick = jnp.where(row == col // (2 * C) + q * MX, 1.0, 0.0).astype(BF)
                terms = dot32(values, pick) * weights
                sums.append(jnp.sum(terms.reshape(MODE_STEP, C, chunk), 1))
            lane = lax.broadcasted_iota(jnp.int32, (MODE_STEP, chunk), 1)
            turn = jnp.where(
                lane % (2 * C) < C, -pltpu.roll(sums[1], chunk - C, 1), pltpu.roll(sums[1], C, 1)
            )
            mixed[pl.ds(first, MODE_STEP), lo : lo + chunk] = sums[0] + turn
        return carry

    lax.fori_loop(0, own * MZ // MODE_STEP, step, 0)
    turned[:, : own * MZ] = mixed[...].T
    for o in range(C):
        piece = turned[pl.ds(o, 2 * MX, stride=C), :]
        for jj in range(own):
            lo = (jj * C + o) * MZ
            rhs[:, lo : lo + MZ] = piece[:, jj * MZ : (jj + 1) * MZ]
    right = rhs[...].astype(BF)
    for p in range(2):
        back = dot32(xi_ref[p], right)
        for t in range(own * tiles):
            flat[pl.ds(p * own * tiles + t, every, stride=slots), :] = back[
                :, t * LANES : (t + 1) * LANES
            ]
    for plane in range(planes):
        send[plane] = (
            flat[plane * count * slots : (plane + 1) * count * slots, :]
            .reshape(count, slots, LANES)
            .astype(BF)
        )


def whole_kernel(
    planes, count, feat_ref, perm_ref, lift_in, lift_out, point, dec_in, dec_out, zf_ref, zi_ref,
    yf_ref, yi_ref, xf_ref, xi_ref, w_hbm, st_ref, cond_ref,
    hid, wbuf, send_f, recv_f, send_b, recv_b, flat, spec, mixed, turned, rhs, zs, zs2, xs, plain,
    in_ref, lo_ref, kp_ref, di_ref, do_ref, w_sem, sf_sem, rf_sem, sb_sem, rb_sem,
):
    me = lax.axis_index("space")
    barrier = pltpu.get_barrier_semaphore()
    for shift in range(1, count):
        pl.semaphore_signal(
            barrier,
            inc=1,
            device_id={"space": lax.rem(me + shift, count)},
            device_id_type=pl.DeviceIdType.MESH,
        )
    fetch = pltpu.make_async_copy(w_hbm.at[0], wbuf, w_sem.at[0])
    fetch.start()
    xs[...] = jnp.zeros_like(xs)
    in_ref[...] = diag_of(lift_in[...], ROWS, 8, 0.5)
    lo_ref[...] = diag_of(lift_out[...], 2, lift_out.shape[0], 1.0)
    for layer in range(LAYERS):
        kp_ref[layer] = diag_of(point[layer], ROWS, C, 0.5)
    di_ref[...] = diag_of(dec_in[...], ROWS, C, 0.5)
    dec = dec_out.shape[0]
    do_ref[...] = spread(
        dec_out[...],
        2 * ROWS,
        ROWS * dec,
        lambda i: i // ROWS,
        lambda j: j % dec,
        lambda i, j: i % ROWS == j // dec,
        1.0,
    )
    pl.semaphore_wait(barrier, count - 1)

    def over(body):
        def run(plane, carry):
            body(plane)
            return carry

        lax.fori_loop(0, planes, run, 0)

    def lift(plane):
        lift_plane(plane, feat_ref, perm_ref, in_ref, lo_ref, zf_ref, hid, plain, xs, zs)
        to_modes(plane, count, yf_ref, zs, flat, send_f)
        send_plane(me, count, plane, send_f, recv_f, sf_sem, rf_sem)

    over(lift)
    for layer in range(LAYERS):
        fetch.wait()
        over(lambda plane: wait_plane(count, plane, recv_f, rf_sem))
        over(lambda plane: wait_plane(count, plane, send_f, sf_sem))
        mix_modes(
            planes, count, recv_f, send_b, wbuf, xf_ref, xi_ref, flat, spec, mixed, turned, rhs
        )
        if layer + 1 < LAYERS:
            fetch = pltpu.make_async_copy(w_hbm.at[layer + 1], wbuf, w_sem.at[layer + 1])
            fetch.start()
        over(lambda plane: send_plane(me, count, plane, send_b, recv_b, sb_sem, rb_sem))

        def rest(plane):
            wait_plane(count, plane, recv_b, rb_sem)
            from_modes(plane, count, recv_b, yi_ref, flat, zs)
            if layer + 1 < LAYERS:
                middle_plane(plane, kp_ref[layer], zi_ref, zf_ref, hid, zs, zs2)
                to_modes(plane, count, yf_ref, zs2, flat, send_f)
                send_plane(me, count, plane, send_f, recv_f, sf_sem, rf_sem)
            else:
                final_plane(
                    plane, kp_ref[layer], zi_ref, di_ref, do_ref, perm_ref, hid, zs, st_ref, cond_ref
                )

        over(rest)
        over(lambda plane: wait_plane(count, plane, send_b, sb_sem))


def ones_where(shape, test, value=1.0):
    row = lax.broadcasted_iota(jnp.int32, shape, 0)
    col = lax.broadcasted_iota(jnp.int32, shape, 1)
    return jnp.where(test(row, col), value, 0.0)


def spread(matrix, rows, cols, row_of, col_of, keep, value):
    take = ones_where((rows, matrix.shape[1]), lambda i, j: row_of(i) == j).astype(BF)
    put = ones_where((matrix.shape[0], cols), lambda i, j: col_of(j) == i).astype(BF)
    part = lax.dot_general(take, matrix, (((1,), (1,)), ((), ())), preferred_element_type=F32)
    return (dot32(part.astype(BF), put) * ones_where((rows, cols), keep, value)).astype(BF)


def diag_of(matrix, copies, width, value):
    depth, height = matrix.shape
    return spread(
        matrix,
        copies * height,
        copies * width,
        lambda i: i % height,
        lambda j: j % width,
        lambda i, j: i // height == j // width,
        value,
    )


def local_fast(
    features,
    log_perm,
    well_cells,
    well_rates,
    lift_in,
    lift_out,
    spec_weight,
    point_weight,
    dec_in,
    dec_out,
):
    planes = features.shape[2]
    count = lax.axis_size("space")
    own = MY // count
    modes = own * MZ
    slots = 2 * modes * C // LANES
    tables = tables_for(count)
    lift, dec = lift_in.shape[1], dec_in.shape[1]
    operands = (
        features,
        log_perm,
        lift_in,
        lift_out,
        point_weight,
        dec_in,
        dec_out,
    ) + tuple(tables[name] for name in ("zf", "zi", "yf", "yi", "xf", "xi"))
    vmem = pl.BlockSpec(memory_space=pltpu.VMEM)
    exchange = pltpu.VMEM((planes, count, slots, LANES), BF)
    states, conduct = pl.pallas_call(
        lambda *refs: whole_kernel(planes, count, *refs),
        in_specs=[vmem] * len(operands) + [pl.BlockSpec(memory_space=pl.ANY)],
        out_specs=[vmem, vmem],
        out_shape=[
            jax.ShapeDtypeStruct((1, 2, planes, NY, NZ), F32),
            jax.ShapeDtypeStruct((1, planes, NY, NZ), F32),
        ],
        scratch_shapes=[
            pltpu.VMEM((planes, PAIRS * C, 2 * NZ), BF),
            pltpu.VMEM(spec_weight.shape[1:], BF),
            exchange,
            exchange,
            exchange,
            exchange,
            pltpu.VMEM((planes * count * slots, LANES), F32),
            pltpu.VMEM((modes * C, LANES), F32),
            pltpu.VMEM((modes, MX * 2 * C), F32),
            pltpu.VMEM((MX * 2 * C, LANES), F32),
            pltpu.VMEM((2 * MX, modes * C), F32),
            pltpu.VMEM((C * PITCH, LANES), F32),
            pltpu.VMEM((C * PITCH, LANES), F32),
            pltpu.VMEM((2, PAIRS * 8, NZ), F32),
            pltpu.VMEM((NY, NZ), F32),
            pltpu.VMEM((ROWS * lift, ROWS * 8), BF),
            pltpu.VMEM((2 * C, 2 * lift), BF),
            pltpu.VMEM((LAYERS, ROWS * C, ROWS * C), BF),
            pltpu.VMEM((ROWS * dec, ROWS * C), BF),
            pltpu.VMEM((2 * ROWS, ROWS * dec), BF),
            pltpu.SemaphoreType.DMA((LAYERS,)),
        ]
        + [pltpu.SemaphoreType.DMA((planes,))] * 4,
        compiler_params=pltpu.CompilerParams(
            collective_id=0, has_side_effects=True, vmem_limit_bytes=60 * 1024 * 1024
        ),
        name="whole",
    )(*operands, spec_weight)
    return (states, darcy(states[:, 0], conduct, well_cells, well_rates))


def local(features, log_perm, well_cells, well_rates, lift_in, lift_out, spec_weight, *rest):
    batches, planes = features.shape[0], features.shape[2]
    count = lax.axis_size("space")
    fits = batches == 1 and planes == 8 and count % 8 == 0 and MY % count == 0
    run = local_fast if fits else local_general
    return run(
        features, log_perm, well_cells, well_rates, lift_in, lift_out, spec_weight, *rest
    )


def solution(mesh):
    return jax.shard_map(
        local,
        mesh=mesh,
        in_specs=(
            P("sample", None, "space", None, None),
            P("sample", "space", None, None),
            P("sample", None),
            P("sample", None),
            P(),
            P(),
            P(None, "space", None, None),
            P(),
            P(),
            P(),
        ),
        out_specs=(P("sample", None, "space", None, None), P("sample", "space", None, None)),
        check_vma=False,
    )
```

profile of v0, /device:TPU:1, one launch (start us, length us, event | category | flops | bytes accessed | tf_op | source)
XLA Modules:
  0.0 188.8 jit_solution(5188556993581537178)
XLA Ops:
  0.6 1.4 copy.21.refs_6_
  2.0 1.4 copy.20.refs_3_
  3.4 170.2 %whole.1 = (f32[1,2,8,128,128]{4,3,2,1,0:T(8,128)}, f32[1,8,128,128]{3,2,1,0:T(8,128)}) custom-call(bf16[1,4,8,128,128]{4,3,2,1,0:T(8,128)(2,1)} %refs_0_.1, f32[1,8,128,128]{3,2,1,0:T(8,128)} %refs_1_.1, bf16[5,128]{1,0:T(8,128)(2,1)} %refs_2_.1, bf16[128,32]{1,0:T(8,128)(2,1)} %copy.20.refs_3_, bf16[2,32,32]{2,1,0:T(8,128)(2,1)} %refs_4_.1, ...), custom_call_target="tpu_custom_call" | custom-call | tf_op jit(solution)/shard_map/whole/pallas_call | solution.py:619
  173.6 0.0 copy-start
  173.6 1.1 convert_bitcast_fusion.4
  174.8 0.0 copy-start.1
  174.8 1.2 fusion.30
  176.0 0.0 copy-start.2
  176.1 3.7 %collective-permute-start = (bf16[1,2,1,128,128]{4,3,2,1,0:T(8,128)(2,1)S(1)}, bf16[1,2,1,128,128]{4,3,2,1,0:T(8,128)(2,1)S(1)}, u32[]{:S(2)}, u32[]{:S(2)}) collective-permute-start(bf16[1,2,1,128,128]{4,3,2,1,0:T(8,128)(2,1)S(1)} %get-tuple-element.16), channel_id=1, source_target_pairs={{0,1},{1,2},{2,3},{3,4},{4,5},{5,6},{6,7},{7,8},{8,9},{9,10},{10,1... | collective-permute-start | bytes 196616 | tf_op jit(solution)/shard_map/ppermute | solution.py:28
  179.8 1.9 %collective-permute-start.1 = (bf16[1,2,1,128,128]{4,3,2,1,0:T(8,128)(2,1)S(1)}, bf16[1,2,1,128,128]{4,3,2,1,0:T(8,128)(2,1)S(1)}, u32[]{:S(2)}, u32[]{:S(2)}) collective-permute-start(bf16[1,2,1,128,128]{4,3,2,1,0:T(8,128)(2,1)S(1)} %get-tuple-element.17), channel_id=1, source_target_pairs={{1,0},{2,1},{3,2},{4,3},{5,4},{6,5},{7,6},{8,7},{9,8},{10,9},{11,1... | collective-permute-start | bytes 196616 | tf_op jit(solution)/shard_map/ppermute | solution.py:31
  181.8 0.0 copy-done
  181.8 0.0 copy-done.1
  181.9 0.0 copy-done.2
  181.9 0.1 fusion.23
  182.0 0.0 copy-start.3
  182.0 0.2 fusion.31
  182.2 0.5 copy-done.3
  182.6 0.1 fusion.22
  182.7 0.1 broadcast_multiply_fusion
  182.8 0.1 maximum_bitcast_fusion
  182.9 0.0 collective-permute-done
  182.9 2.5 %collective-permute-done.1 = bf16[1,2,1,128,128]{4,3,2,1,0:T(8,128)(2,1)S(1)} collective-permute-done((bf16[1,2,1,128,128]{4,3,2,1,0:T(8,128)(2,1)S(1)}, bf16[1,2,1,128,128]{4,3,2,1,0:T(8,128)(2,1)S(1)}, u32[]{:S(2)}, u32[]{:S(2)}) %collective-permute-start.1) | collective-permute-done | bytes 65568 | tf_op jit(solution)/shard_map/ppermute | solution.py:31
  185.4 2.4 %fusion = f32[1,8,128,128]{3,2,1,0:T(8,128)} fusion(f32[1,8,128,128]{3,2,1,0:T(8,128)S(1)} %slice_bitcast_fusion, f32[1,7,128,128]{3,2,1,0:T(8,128)S(1)} %get-tuple-element.21, f32[1,1,128,128]{3,2,1,0:T(8,128)S(1)} %get-tuple-element.10, f32[1,1,128,128]{3,2,1,0:T(8,128)S(1)} %get-tuple-element.11, f32[1,7,128,128]{3,2,1,0:T(8,128)S(1)} %get-tuple-element.22, ...), kind=kOutput, calls=%fused_computation.9 | convolution fusion | flops 55709696 | bytes 3801216 | tf_op jit(solution)/shard_map/bwa,bwz->baz/dot_general | solution.py:133
  187.8 1.0 copy.33
  (5 shorter events, 0.1 us)
Async XLA Ops:
  173.6 8.1 %copy-start = (f32[1,8,128,128]{3,2,1,0:T(8,128)S(1)}, f32[1,8,128,128]{3,2,1,0:T(8,128)}, u32[]{:S(2)}) copy-start(f32[1,8,128,128]{3,2,1,0:T(8,128)} %get-tuple-element.5) | copy-start | bytes 1572868
  174.8 7.0 %copy-start.1 = (f32[1,2,8,128,128]{4,3,2,1,0:T(8,128)S(1)}, f32[1,2,8,128,128]{4,3,2,1,0:T(8,128)}, u32[]{:S(2)}) copy-start(f32[1,2,8,128,128]{4,3,2,1,0:T(8,128)} %get-tuple-element.25) | copy-start | bytes 3145732
  176.0 5.8 %copy-start.2 = (s32[1,32]{1,0:T(1,128)S(1)}, s32[1,32]{1,0:T(1,128)}, u32[]{:S(2)}) copy-start(s32[1,32]{1,0:T(1,128)} %param.18) | copy-start | bytes 388
  176.1 6.8 %collective-permute-start = (bf16[1,2,1,128,128]{4,3,2,1,0:T(8,128)(2,1)S(1)}, bf16[1,2,1,128,128]{4,3,2,1,0:T(8,128)(2,1)S(1)}, u32[]{:S(2)}, u32[]{:S(2)}) collective-permute-start(bf16[1,2,1,128,128]{4,3,2,1,0:T(8,128)(2,1)S(1)} %get-tuple-element.16), channel_id=1, source_target_pairs={{0,1},{1,2},{2,3},{3,4},{4,5},{5,6},{6,7},{7,8},{8,9},{9,10},{10,1... | collective-permute-start | bytes 196616 | tf_op jit(solution)/shard_map/ppermute | solution.py:28
  179.8 5.6 %collective-permute-start.1 = (bf16[1,2,1,128,128]{4,3,2,1,0:T(8,128)(2,1)S(1)}, bf16[1,2,1,128,128]{4,3,2,1,0:T(8,128)(2,1)S(1)}, u32[]{:S(2)}, u32[]{:S(2)}) collective-permute-start(bf16[1,2,1,128,128]{4,3,2,1,0:T(8,128)(2,1)S(1)} %get-tuple-element.17), channel_id=1, source_target_pairs={{1,0},{2,1},{3,2},{4,3},{5,4},{6,5},{7,6},{8,7},{9,8},{10,9},{11,1... | collective-permute-start | bytes 196616 | tf_op jit(solution)/shard_map/ppermute | solution.py:31
  182.0 0.7 copy-start.3
where the time goes:
time: 189 us
  Pallas kernels  170 us (90%)
  local copies, waits for them, and re-layouts  5.67 us (3%)
  starting transfers between devices  5.66 us (3%)
  waiting for transfers between devices  2.53 us (1%)
  matrix products  2.37 us (1%)
    pallas_call x1, Pallas kernels, local_fast(): pl.pallas_call(lambda *refs: whole_kernel(planes, count, *refs), in_specs...  170 us
    unnamed x11, local copies, waits for them, and re-layouts  4.21 us
  transfers between devices with their start and end apart: 2, of which 1 were waited for; matrix products, arithmetic and copies ran while one was open for 0% of the time, Pallas kernels for 0%

commit v1 on v0

--- a/solution.py
+++ b/solution.py
@@ -214,10 +214,12 @@
 BF = jnp.bfloat16
 F32 = jnp.float32
 PAIRS = NY // 2
-PITCH = PAIRS + 8
+SKEW = 4
+PITCH = PAIRS + SKEW
 MODE_STEP = 8
 ROWS = 8
 UNROLL = 4
+LIFT_UNROLL = 4
 LANES = 128
 
 
@@ -259,8 +261,8 @@
         "zi": 0.5 * np.kron(pair, z_inverse),
         "yf": y_forward.transpose(3, 5, 4, 1, 2, 0).reshape(2 * MY, 2 * NY),
         "yi": y_inverse.transpose(5, 3, 4, 2, 1, 0).reshape(2 * NY, 2 * MY),
-        "xf": by_plane(np_forward(NX, MX).transpose(1, 2, 3, 0).reshape(2, 2 * MX, NX), 2, count),
-        "xi": by_plane(np_inverse(NX, MX).transpose(2, 3, 0, 1).reshape(2, NX, 2 * MX), 1, count),
+        "xf": by_plane(np_forward(NX, MX).transpose(2, 3, 1, 0), 3, count).reshape(2 * MX, 2 * NX),
+        "xi": by_plane(np_inverse(NX, MX).transpose(2, 3, 0, 1), 1, count).reshape(2 * NX, 2 * MX),
     }
     return {name: jnp.asarray(table.astype(np.float32)).astype(BF) for name, table in tables.items()}
 
@@ -325,10 +327,11 @@
     slots = 2 * MY // count * tiles
     for s in range(2 * MY // count):
         for t in range(tiles):
-            flat[pl.ds(s * tiles + t, count, stride=slots), :] = modes[
+            flat[pl.ds(s * tiles + t, count, stride=slots + SKEW), :] = modes[
                 s * count : (s + 1) * count, t * LANES : (t + 1) * LANES
             ]
-    send[plane] = flat[: count * slots, :].reshape(count, slots, LANES).astype(BF)
+    for dst in range(count):
+        send[plane, dst] = flat[pl.ds(dst * (slots + SKEW), slots), :].astype(BF)
 
 
 def lay_out(zs, start, values):
@@ -346,32 +349,44 @@
         for y2 in range(2):
             xs[y2, pl.ds(f, PAIRS, stride=8), :] = plain[pl.ds(y2, PAIRS, stride=2), :]
     width = lo_ref.shape[1]
-
-    def block(index, carry):
-        start = pl.multiple_of(index * ROWS * 8, ROWS * 8)
-        x = jnp.concatenate([xs[0, pl.ds(start, ROWS * 8), :], xs[1, pl.ds(start, ROWS * 8), :]], 1)
-        lifted = gelu_of_half(dot32(in_ref[...], x.astype(BF)))
-        parts = [
-            dot32(lo_ref[...], lifted[r * width : (r + 1) * width, :]).astype(BF)
-            for r in range(lifted.shape[0] // width)
-        ]
-        hidden = jnp.concatenate(parts, 0)
-        hid[plane, hid_rows(index), :] = hidden
-        lay_out(zs, index * ROWS, dot32(hidden, zf_ref[...]))
+    parts = in_ref.shape[0] // width
+
+    def group(step, carry):
+        base = step * LIFT_UNROLL
+
+        def first(n):
+            u, r = n // parts, n % parts
+            start = pl.multiple_of((base + u) * ROWS * 8, ROWS * 8)
+            x = jnp.concatenate([xs[y2, pl.ds(start, ROWS * 8), :] for y2 in range(2)], 1)
+            return dot32(in_ref[r * width : (r + 1) * width, :], x.astype(BF))
+
+        now = first(0)
+        done = []
+        for n in range(LIFT_UNROLL * parts):
+            later = first(n + 1) if n + 1 < LIFT_UNROLL * parts else None
+            done.append(dot32(lo_ref[...], gelu_of_half(now)).astype(BF))
+            now = later
+            if len(done) == parts:
+                index = base + n // parts
+                hidden = jnp.concatenate(done, 0)
+                done = []
+                hid[plane, hid_rows(index), :] = hidden
+                lay_out(zs, index * ROWS, dot32(hidden, zf_ref[...]))
         return carry
 
-    lax.fori_loop(0, PAIRS // ROWS, block, 0, unroll=UNROLL)
+    lax.fori_loop(0, PAIRS // ROWS // LIFT_UNROLL, group, 0)
 
 
 def from_modes(plane, count, recv, yi_ref, flat, zs):
     tiles = C * MZ // LANES
     slots = 2 * MY // count * tiles
-    flat[: count * slots, :] = recv[plane].astype(F32).reshape(count * slots, LANES)
+    for src in range(count):
+        flat[pl.ds(src * (slots + SKEW), slots), :] = recv[plane, src].astype(F32)
     rows = []
     for s in range(2 * MY // count):
         rows.append(
             jnp.concatenate(
-                [flat[pl.ds(s * tiles + t, count, stride=slots), :] for t in range(tiles)], 1
+                [flat[pl.ds(s * tiles + t, count, stride=slots + SKEW), :] for t in range(tiles)], 1
             ).astype(BF)
         )
     back = dot32(yi_ref[...], jnp.concatenate(rows, 0))
@@ -416,78 +431,116 @@
     cond_ref[0, plane] = mobility_of(sat, perm_ref[0, plane])
 
 
-def mix_modes(planes, count, recv, send, wbuf, xf_ref, xi_ref, flat, spec, mixed, turned, rhs):
+def mix_modes(planes, count, recv, send, wbuf, xf_ref, xi_ref, flat, spec, rows, mixed, turned):
     own = MY // count
     tiles = C * MZ // LANES
     slots = 2 * own * tiles
+    pitch = slots + SKEW
     every = count * planes
-    wide = MX * 2 * C
-    for plane in range(planes):
-        flat[plane * count * slots : (plane + 1) * count * slots, :] = (
-            recv[plane].astype(F32).reshape(count * slots, LANES)
-        )
-    total = 0.0
-    for p in range(2):
+    lane = lax.broadcasted_iota(jnp.int32, (1, LANES), 1)
+    low = lane < 64
+    even = lane % 64 < 32
+
+    def unpack(plane, carry):
+        for src in range(count):
+            start = (plane * count + src) * pitch
+            flat[pl.ds(start, slots), :] = recv[plane, src].astype(F32)
+        return carry
+
+    lax.fori_loop(0, planes, unpack, 0)
+
+    def column(p, t):
+        return flat[pl.ds(p * own * tiles + t, every, stride=pitch), :].astype(BF)
+
+    for pair in range(own * tiles // 2):
         right = jnp.concatenate(
             [
-                flat[pl.ds(p * own * tiles + t, every, stride=slots), :].astype(BF)
-                for t in range(own * tiles)
+                jnp.concatenate([column(p, pair * 2 + half) for half in range(2)], 1)
+                for p in range(2)
             ],
-            1,
-        )
-        total = total + dot32(xf_ref[p], right)
-    spec[:, : 2 * MX] = total.T
-    chunk = 512
-
-    def step(index, carry):
-        first = pl.multiple_of(index * MODE_STEP, MODE_STEP)
-        base = first // MZ * (C * MZ) + first % MZ
-        rows = [spec[pl.ds(base + r, C, stride=MZ), :] for r in range(MODE_STEP)]
-        values = jnp.concatenate(rows, 0)[:, : 2 * MX].astype(BF)
-        for piece in range(wide // chunk):
-            lo = piece * chunk
-            row = lax.broadcasted_iota(jnp.int32, (2 * MX, chunk), 0)
-            col = lax.broadcasted_iota(jnp.int32, (2 * MX, chunk), 1) + lo
-            weights = wbuf[pl.ds(first, MODE_STEP), :, lo : lo + chunk]
-            weights = weights.reshape(MODE_STEP * C, chunk).astype(F32)
-            sums = []
-            for q in range(2):
-                pick = jnp.where(row == col // (2 * C) + q * MX, 1.0, 0.0).astype(BF)
-                terms = dot32(values, pick) * weights
-                sums.append(jnp.sum(terms.reshape(MODE_STEP, C, chunk), 1))
-            lane = lax.broadcasted_iota(jnp.int32, (MODE_STEP, chunk), 1)
-            turn = jnp.where(
-                lane % (2 * C) < C, -pltpu.roll(sums[1], chunk - C, 1), pltpu.roll(sums[1], C, 1)
-            )
-            mixed[pl.ds(first, MODE_STEP), lo : lo + chunk] = sums[0] + turn
+            0,
+        )
+        total = dot32(xf_ref[...], right)
+        for half in range(2):
+            part = total[:, half * LANES : (half + 1) * LANES].T
+            for r in range(4):
+                first = (pair * 2 + half) * 4 + r
+                spec[pl.ds(first * (MZ + SKEW), MZ), : 2 * MX] = part[r * MZ : (r + 1) * MZ, :]
+    groups = own * MZ // MODE_STEP
+    for group in range(groups):
+        jj, k = group * MODE_STEP // MZ, group * MODE_STEP % MZ
+        base = jj * C * (MZ + SKEW) + k
+        picked = [
+            spec[pl.ds(base + r, C, stride=MZ + SKEW), : 2 * MX] for r in range(MODE_STEP)
+        ]
+        rows[group] = jnp.concatenate(picked, 0).T
+    wide = MODE_STEP * C
+    own_mode = lax.broadcasted_iota(jnp.int32, (MODE_STEP, wide), 0) == (
+        lax.broadcasted_iota(jnp.int32, (MODE_STEP, wide), 1) // C
+    )
+    per = wide // (2 * C)
+
+    def step(group, carry):
+        first = pl.multiple_of(group * MODE_STEP, MODE_STEP)
+        for piece in range(MX // per):
+            left = []
+            for i in range(per):
+                for q in range(2):
+                    row = rows[group, pl.ds(q * MX + piece * per + i, MODE_STEP, stride=0), :]
+                    left.append(jnp.where(own_mode, row, 0.0))
+            lo = piece * wide
+            weights = wbuf[pl.ds(first, MODE_STEP), :, lo : lo + wide].reshape(wide, wide)
+            both = dot32(jnp.concatenate(left, 0).astype(BF), weights)
+
+            def part(i, q, t):
+                at = (i * 2 + q) * MODE_STEP
+                return both[at : at + MODE_STEP, t * LANES : (t + 1) * LANES]
+
+            for t in range(2):
+                real, imag = (
+                    jnp.where(low, part(2 * t, q, t), part(2 * t + 1, q, t)) for q in range(2)
+                )
+                turn = jnp.where(even, -pltpu.roll(imag, LANES - C, 1), pltpu.roll(imag, C, 1))
+                mixed[pl.ds(first, MODE_STEP), lo + t * LANES : lo + (t + 1) * LANES] = real + turn
         return carry
 
-    lax.fori_loop(0, own * MZ // MODE_STEP, step, 0)
-    turned[:, : own * MZ] = mixed[...].T
-    for o in range(C):
-        piece = turned[pl.ds(o, 2 * MX, stride=C), :]
+    lax.fori_loop(0, groups, step, 0)
+    for block in range(MX * 2 * C // LANES):
+        part = mixed[:, block * LANES : (block + 1) * LANES].T
+        for r in range(4):
+            first = (block * 4 + r) * (C + SKEW)
+            turned[pl.ds(first, C), : own * MZ] = part[r * C : (r + 1) * C, :]
+    for pair in range(tiles // 2):
+        right = [[], []]
+        for half in range(2):
+            o = (pair * 2 + half) * 4
+            a = [turned[pl.ds(o + r, 2 * MX, stride=C + SKEW), :] for r in range(4)]
+            b = jnp.where(low, a[0], pltpu.roll(a[2], 64, 1))
+            c = jnp.where(low, a[1], pltpu.roll(a[3], 64, 1))
+            right[0].append(jnp.where(even, b, pltpu.roll(c, 32, 1)))
+            right[1].append(jnp.where(even, pltpu.roll(b, LANES - 32, 1), c))
         for jj in range(own):
-            lo = (jj * C + o) * MZ
-            rhs[:, lo : lo + MZ] = piece[:, jj * MZ : (jj + 1) * MZ]
-    right = rhs[...].astype(BF)
-    for p in range(2):
-        back = dot32(xi_ref[p], right)
-        for t in range(own * tiles):
-            flat[pl.ds(p * own * tiles + t, every, stride=slots), :] = back[
-                :, t * LANES : (t + 1) * LANES
-            ]
-    for plane in range(planes):
-        send[plane] = (
-            flat[plane * count * slots : (plane + 1) * count * slots, :]
-            .reshape(count, slots, LANES)
-            .astype(BF)
-        )
+            back = dot32(xi_ref[...], jnp.concatenate(right[jj], 1).astype(BF))
+            for p in range(2):
+                for half in range(2):
+                    slot = (p * own + jj) * tiles + pair * 2 + half
+                    flat[pl.ds(slot, every, stride=pitch), :] = back[
+                        p * every : (p + 1) * every, half * LANES : (half + 1) * LANES
+                    ]
+
+    def pack(plane, carry):
+        for dst in range(count):
+            start = (plane * count + dst) * pitch
+            send[plane, dst] = flat[pl.ds(start, slots), :].astype(BF)
+        return carry
+
+    lax.fori_loop(0, planes, pack, 0)
 
 
 def whole_kernel(
     planes, count, feat_ref, perm_ref, lift_in, lift_out, point, dec_in, dec_out, zf_ref, zi_ref,
     yf_ref, yi_ref, xf_ref, xi_ref, w_hbm, st_ref, cond_ref,
-    hid, wbuf, send_f, recv_f, send_b, recv_b, flat, spec, mixed, turned, rhs, zs, zs2, xs, plain,
+    hid, wbuf, send_f, recv_f, send_b, recv_b, flat, spec, rows, mixed, turned, zs, zs2, xs, plain,
     in_ref, lo_ref, kp_ref, di_ref, do_ref, w_sem, sf_sem, rf_sem, sb_sem, rb_sem,
 ):
     me = lax.axis_index("space")
@@ -503,11 +556,11 @@
     fetch.start()
     xs[...] = jnp.zeros_like(xs)
     in_ref[...] = diag_of(lift_in[...], ROWS, 8, 0.5)
-    lo_ref[...] = diag_of(lift_out[...], 2, lift_out.shape[0], 1.0)
+    lo_ref[...] = diag_of(lift_out[...], 2, lift_out.shape[1], 1.0, True)
     for layer in range(LAYERS):
         kp_ref[layer] = diag_of(point[layer], ROWS, C, 0.5)
     di_ref[...] = diag_of(dec_in[...], ROWS, C, 0.5)
-    dec = dec_out.shape[0]
+    dec = dec_out.shape[1]
     do_ref[...] = spread(
         dec_out[...],
         2 * ROWS,
@@ -516,6 +569,7 @@
         lambda j: j % dec,
         lambda i, j: i % ROWS == j // dec,
         1.0,
+        True,
     )
     pl.semaphore_wait(barrier, count - 1)
 
@@ -537,7 +591,7 @@
         over(lambda plane: wait_plane(count, plane, recv_f, rf_sem))
         over(lambda plane: wait_plane(count, plane, send_f, sf_sem))
         mix_modes(
-            planes, count, recv_f, send_b, wbuf, xf_ref, xi_ref, flat, spec, mixed, turned, rhs
+            planes, count, recv_f, send_b, wbuf, xf_ref, xi_ref, flat, spec, rows, mixed, turned
         )
         if layer + 1 < LAYERS:
             fetch = pltpu.make_async_copy(w_hbm.at[layer + 1], wbuf, w_sem.at[layer + 1])
@@ -566,15 +620,17 @@
     return jnp.where(test(row, col), value, 0.0)
 
 
-def spread(matrix, rows, cols, row_of, col_of, keep, value):
-    take = ones_where((rows, matrix.shape[1]), lambda i, j: row_of(i) == j).astype(BF)
-    put = ones_where((matrix.shape[0], cols), lambda i, j: col_of(j) == i).astype(BF)
-    part = lax.dot_general(take, matrix, (((1,), (1,)), ((), ())), preferred_element_type=F32)
+def spread(matrix, rows, cols, row_of, col_of, keep, value, turned):
+    depth, height = matrix.shape[::-1] if turned else matrix.shape
+    take = ones_where((rows, height), lambda i, j: row_of(i) == j).astype(BF)
+    put = ones_where((depth, cols), lambda i, j: col_of(j) == i).astype(BF)
+    dims = (((1,), (0 if turned else 1,)), ((), ()))
+    part = lax.dot_general(take, matrix, dims, preferred_element_type=F32)
     return (dot32(part.astype(BF), put) * ones_where((rows, cols), keep, value)).astype(BF)
 
 
-def diag_of(matrix, copies, width, value):
-    depth, height = matrix.shape
+def diag_of(matrix, copies, width, value, turned=False):
+    height = matrix.shape[0 if turned else 1]
     return spread(
         matrix,
         copies * height,
@@ -583,6 +639,7 @@
         lambda j: j % width,
         lambda i, j: i // height == j // width,
         value,
+        turned,
     )
 
 
@@ -609,10 +666,10 @@
         features,
         log_perm,
         lift_in,
-        lift_out,
+        lift_out.T,
         point_weight,
         dec_in,
-        dec_out,
+        dec_out.T,
     ) + tuple(tables[name] for name in ("zf", "zi", "yf", "yi", "xf", "xi"))
     vmem = pl.BlockSpec(memory_space=pltpu.VMEM)
     exchange = pltpu.VMEM((planes, count, slots, LANES), BF)
@@ -631,11 +688,11 @@
             exchange,
             exchange,
             exchange,
-            pltpu.VMEM((planes * count * slots, LANES), F32),
-            pltpu.VMEM((modes * C, LANES), F32),
+            pltpu.VMEM((planes * count * (slots + SKEW), LANES), F32),
+            pltpu.VMEM((own * C * (MZ + SKEW), LANES), F32),
+            pltpu.VMEM((modes // MODE_STEP, 2 * MX, MODE_STEP * C), F32),
             pltpu.VMEM((modes, MX * 2 * C), F32),
-            pltpu.VMEM((MX * 2 * C, LANES), F32),
-            pltpu.VMEM((2 * MX, modes * C), F32),
+            pltpu.VMEM((2 * MX * (C + SKEW), LANES), F32),
             pltpu.VMEM((C * PITCH, LANES), F32),
             pltpu.VMEM((C * PITCH, LANES), F32),
             pltpu.VMEM((2, PAIRS * 8, NZ), F32),
@@ -659,7 +716,7 @@
 def local(features, log_perm, well_cells, well_rates, lift_in, lift_out, spec_weight, *rest):
     batches, planes = features.shape[0], features.shape[2]
     count = lax.axis_size("space")
-    fits = batches == 1 and planes == 8 and count % 8 == 0 and MY % count == 0
+    fits = batches == 1 and planes == 8 and count % 8 == 0 and MY == 2 * count
     run = local_fast if fits else local_general
     return run(
         features, log_perm, well_cells, well_rates, lift_in, lift_out, spec_weight, *rest

time: 189 us -> 169 us (0.89)
  Pallas kernels: 170 us -> 153 us
  local copies, waits for them, and re-layouts: 5.67 us -> 2.9 us
    pallas_call x1, Pallas kernels: 170 us -> 153 us  [local_fast(): pl.pallas_call(lambda *refs: whole_kernel(planes, count, *refs), in_specs...]
    unnamed x11 -> x9, local copies, waits for them, and re-layouts: 4.21 us -> 1.44 us
where the time goes in v1:
time: 169 us
  Pallas kernels  153 us (91%)
  starting transfers between devices  5.72 us (3%)
  local copies, waits for them, and re-layouts  2.9 us (2%)
  waiting for transfers between devices  2.53 us (1%)
  matrix products  2.38 us (1%)
    pallas_call x1, Pallas kernels, local_fast(): pl.pallas_call(lambda *refs: whole_kernel(planes, count, *refs), in_specs...  153 us
    ppermute x1, starting transfers between devices, padded_2(): lax.ppermute(lax.slice_in_dim(block, block.shape[dim] - width, None, axis...  3.8 us
  transfers between devices with their start and end apart: 2, of which 1 were waited for; matrix products, arithmetic and copies ran while one was open for 0% of the time, Pallas kernels for 0%

profile of v1, /device:TPU:1, one launch (start us, length us, event | category | flops | bytes accessed | tf_op | source)
XLA Modules:
  0.0 168.6 jit_solution(17379373061433405579)
XLA Ops:
  0.6 152.8 %whole.1 = (f32[1,2,8,128,128]{4,3,2,1,0:T(8,128)}, f32[1,8,128,128]{3,2,1,0:T(8,128)}) custom-call(bf16[1,4,8,128,128]{4,3,2,1,0:T(8,128)(2,1)} %refs_0_.1, f32[1,8,128,128]{3,2,1,0:T(8,128)} %refs_1_.1, bf16[5,128]{1,0:T(8,128)(2,1)} %refs_2_.1, bf16[32,128]{1,0:T(8,128)(2,1)} %bitcast.48, bf16[2,32,32]{2,1,0:T(8,128)(2,1)} %refs_4_.1, ...), custom_call_target="tpu_custom_call" | custom-call | tf_op jit(solution)/shard_map/whole/pallas_call | solution.py:676
  153.4 0.0 copy-start
  153.4 1.1 convert_bitcast_fusion.4
  154.6 0.0 copy-start.1
  154.6 1.2 fusion.30
  155.8 0.0 copy-start.2
  155.9 3.8 %collective-permute-start = (bf16[1,2,1,128,128]{4,3,2,1,0:T(8,128)(2,1)S(1)}, bf16[1,2,1,128,128]{4,3,2,1,0:T(8,128)(2,1)S(1)}, u32[]{:S(2)}, u32[]{:S(2)}) collective-permute-start(bf16[1,2,1,128,128]{4,3,2,1,0:T(8,128)(2,1)S(1)} %get-tuple-element.16), channel_id=1, source_target_pairs={{0,1},{1,2},{2,3},{3,4},{4,5},{5,6},{6,7},{7,8},{8,9},{9,10},{10,1... | collective-permute-start | bytes 196616 | tf_op jit(solution)/shard_map/ppermute | solution.py:28
  159.7 1.9 %collective-permute-start.1 = (bf16[1,2,1,128,128]{4,3,2,1,0:T(8,128)(2,1)S(1)}, bf16[1,2,1,128,128]{4,3,2,1,0:T(8,128)(2,1)S(1)}, u32[]{:S(2)}, u32[]{:S(2)}) collective-permute-start(bf16[1,2,1,128,128]{4,3,2,1,0:T(8,128)(2,1)S(1)} %get-tuple-element.17), channel_id=1, source_target_pairs={{1,0},{2,1},{3,2},{4,3},{5,4},{6,5},{7,6},{8,7},{9,8},{10,9},{11,1... | collective-permute-start | bytes 196616 | tf_op jit(solution)/shard_map/ppermute | solution.py:31
  161.6 0.0 copy-done
  161.7 0.0 copy-done.1
  161.7 0.0 copy-done.2
  161.8 0.1 fusion.23
  161.8 0.0 copy-start.3
  161.8 0.2 fusion.31
  162.0 0.5 copy-done.3
  162.5 0.1 fusion.22
  162.6 0.1 broadcast_multiply_fusion
  162.7 0.1 maximum_bitcast_fusion
  162.7 0.0 collective-permute-done
  162.7 2.5 %collective-permute-done.1 = bf16[1,2,1,128,128]{4,3,2,1,0:T(8,128)(2,1)S(1)} collective-permute-done((bf16[1,2,1,128,128]{4,3,2,1,0:T(8,128)(2,1)S(1)}, bf16[1,2,1,128,128]{4,3,2,1,0:T(8,128)(2,1)S(1)}, u32[]{:S(2)}, u32[]{:S(2)}) %collective-permute-start.1) | collective-permute-done | bytes 65568 | tf_op jit(solution)/shard_map/ppermute | solution.py:31
  165.3 2.4 %fusion = f32[1,8,128,128]{3,2,1,0:T(8,128)} fusion(f32[1,8,128,128]{3,2,1,0:T(8,128)S(1)} %slice_bitcast_fusion, f32[1,7,128,128]{3,2,1,0:T(8,128)S(1)} %get-tuple-element.21, f32[1,1,128,128]{3,2,1,0:T(8,128)S(1)} %get-tuple-element.10, f32[1,1,128,128]{3,2,1,0:T(8,128)S(1)} %get-tuple-element.11, f32[1,7,128,128]{3,2,1,0:T(8,128)S(1)} %get-tuple-element.22, ...), kind=kOutput, calls=%fused_computation.9 | convolution fusion | flops 55709696 | bytes 3801216 | tf_op jit(solution)/shard_map/bwa,bwz->baz/dot_general | solution.py:133
  167.7 1.0 copy.29
  (5 shorter events, 0.1 us)
Async XLA Ops:
  153.4 8.2 %copy-start = (f32[1,8,128,128]{3,2,1,0:T(8,128)S(1)}, f32[1,8,128,128]{3,2,1,0:T(8,128)}, u32[]{:S(2)}) copy-start(f32[1,8,128,128]{3,2,1,0:T(8,128)} %get-tuple-element.5) | copy-start | bytes 1572868
  154.6 7.1 %copy-start.1 = (f32[1,2,8,128,128]{4,3,2,1,0:T(8,128)S(1)}, f32[1,2,8,128,128]{4,3,2,1,0:T(8,128)}, u32[]{:S(2)}) copy-start(f32[1,2,8,128,128]{4,3,2,1,0:T(8,128)} %get-tuple-element.25) | copy-start | bytes 3145732
  155.8 5.9 %copy-start.2 = (s32[1,32]{1,0:T(1,128)S(1)}, s32[1,32]{1,0:T(1,128)}, u32[]{:S(2)}) copy-start(s32[1,32]{1,0:T(1,128)} %param.18) | copy-start | bytes 388
  155.9 6.9 %collective-permute-start = (bf16[1,2,1,128,128]{4,3,2,1,0:T(8,128)(2,1)S(1)}, bf16[1,2,1,128,128]{4,3,2,1,0:T(8,128)(2,1)S(1)}, u32[]{:S(2)}, u32[]{:S(2)}) collective-permute-start(bf16[1,2,1,128,128]{4,3,2,1,0:T(8,128)(2,1)S(1)} %get-tuple-element.16), channel_id=1, source_target_pairs={{0,1},{1,2},{2,3},{3,4},{4,5},{5,6},{6,7},{7,8},{8,9},{9,10},{10,1... | collective-permute-start | bytes 196616 | tf_op jit(solution)/shard_map/ppermute | solution.py:28
  159.7 5.6 %collective-permute-start.1 = (bf16[1,2,1,128,128]{4,3,2,1,0:T(8,128)(2,1)S(1)}, bf16[1,2,1,128,128]{4,3,2,1,0:T(8,128)(2,1)S(1)}, u32[]{:S(2)}, u32[]{:S(2)}) collective-permute-start(bf16[1,2,1,128,128]{4,3,2,1,0:T(8,128)(2,1)S(1)} %get-tuple-element.17), channel_id=1, source_target_pairs={{1,0},{2,1},{3,2},{4,3},{5,4},{6,5},{7,6},{8,7},{9,8},{10,9},{11,1... | collective-permute-start | bytes 196616 | tf_op jit(solution)/shard_map/ppermute | solution.py:31
  161.8 0.7 copy-start.3

commit v2 on v1

--- a/solution.py
+++ b/solution.py
@@ -218,8 +218,9 @@
 PITCH = PAIRS + SKEW
 MODE_STEP = 8
 ROWS = 8
-UNROLL = 4
-LIFT_UNROLL = 4
+LOOK = 4
+LAG = 1
+MID = 2
 LANES = 128
 
 
@@ -255,10 +256,12 @@
     z_inverse = np.concatenate([twice * cosine, -twice * sine], 0)
     y_forward = np_forward(NY, MY).reshape(PAIRS, 2, 2, 2, count, own)
     y_inverse = np_inverse(NY, MY).reshape(count, own, 2, 2, PAIRS, 2)
-    pair = np.eye(2)
+    four = np.eye(4)
+    z_forward = np.einsum("zpk,cd->czpdk", z_forward.reshape(NZ, 2, MZ), four)
+    z_inverse = np.einsum("pkz,cd->pckdz", z_inverse.reshape(2, MZ, NZ), four)
     tables = {
-        "zf": np.kron(pair, z_forward),
-        "zi": 0.5 * np.kron(pair, z_inverse),
+        "zf": z_forward.reshape(4 * NZ, 8 * MZ),
+        "zi": 0.5 * z_inverse.reshape(8 * MZ, 4 * NZ),
         "yf": y_forward.transpose(3, 5, 4, 1, 2, 0).reshape(2 * MY, 2 * NY),
         "yi": y_inverse.transpose(5, 3, 4, 2, 1, 0).reshape(2 * NY, 2 * MY),
         "xf": by_plane(np_forward(NX, MX).transpose(2, 3, 1, 0), 3, count).reshape(2 * MX, 2 * NX),
@@ -276,26 +279,6 @@
     scale = math.sqrt(2.0 / math.pi)
     inner = u * (BF(2.0 * scale) + BF(8.0 * scale * 0.044715) * (u * u))
     return u + u * jnp.tanh(inner)
-
-
-def swap_blocks(four):
-    shape = four[0].shape
-    lane = lax.broadcasted_iota(jnp.int32, shape, 1)
-    low = lane < 64
-    even = lane % 64 < 32
-    a0, a1, a2, a3 = four
-
-    def cross(a, b, keep, shift):
-        return (
-            jnp.where(keep, a, pltpu.roll(b, shift, 1)),
-            jnp.where(keep, pltpu.roll(a, LANES - shift, 1), b),
-        )
-
-    b0, b2 = cross(a0, a2, low, 64)
-    b1, b3 = cross(a1, a3, low, 64)
-    c0, c1 = cross(b0, b1, even, 32)
-    c2, c3 = cross(b2, b3, even, 32)
-    return c0, c1, c2, c3
 
 
 def send_plane(me, count, plane, send, recv, send_sem, recv_sem):
@@ -317,115 +300,148 @@
     pltpu.make_async_copy(part, part, sem.at[plane]).wait()
 
 
-def to_modes(plane, count, yf_ref, zs, flat, send):
-    pieces = []
-    for group in range(C // 4):
-        four = [zs[(group * 4 + r) * PITCH : (group * 4 + r) * PITCH + PAIRS, :] for r in range(4)]
-        pieces.append(jnp.concatenate([p.astype(BF) for p in swap_blocks(four)], 0))
-    modes = dot32(yf_ref[...], jnp.concatenate(pieces, 1))
+def to_modes(plane, count, zf_ref, yf_ref, zs, flat, send):
     tiles = C * MZ // LANES
     slots = 2 * MY // count * tiles
-    for s in range(2 * MY // count):
-        for t in range(tiles):
-            flat[pl.ds(s * tiles + t, count, stride=slots + SKEW), :] = modes[
-                s * count : (s + 1) * count, t * LANES : (t + 1) * LANES
-            ]
+    for pair in range(tiles // 2):
+        columns = []
+        for group in (pair * 2, pair * 2 + 1):
+            halves = []
+            for y2 in range(2):
+                left = [zs[y2, pl.ds((group * 4 + r) * PITCH, PAIRS), :] for r in range(4)]
+                halves.append(dot32(jnp.concatenate(left, 1).astype(BF), zf_ref[...]).astype(BF))
+            parts = [half[:, p * LANES : (p + 1) * LANES] for half in halves for p in range(2)]
+            columns.append(jnp.concatenate(parts, 0))
+        modes = dot32(yf_ref[...], jnp.concatenate(columns, 1))
+        for s in range(2 * MY // count):
+            for half in range(2):
+                flat[pl.ds(s * tiles + pair * 2 + half, count, stride=slots + SKEW), :] = modes[
+                    s * count : (s + 1) * count, half * LANES : (half + 1) * LANES
+                ]
     for dst in range(count):
         send[plane, dst] = flat[pl.ds(dst * (slots + SKEW), slots), :].astype(BF)
 
 
 def lay_out(zs, start, values):
-    for r in range(ROWS):
-        zs[pl.ds(start + r, C, stride=PITCH), :] = values[r * C : (r + 1) * C, :]
+    for y2 in range(2):
+        for r in range(ROWS):
+            zs[y2, pl.ds(start + r, C, stride=PITCH), :] = values[
+                r * C : (r + 1) * C, y2 * NZ : (y2 + 1) * NZ
+            ]
 
 
 def hid_rows(index):
-    return pl.ds(pl.multiple_of(index * ROWS * C, ROWS * C), ROWS * C)
-
-
-def lift_plane(plane, feat_ref, perm_ref, in_ref, lo_ref, zf_ref, hid, plain, xs, zs):
+    return pl.ds(index * ROWS * C, ROWS * C)
+
+
+def lift_plane(plane, feat_ref, perm_ref, in_ref, lo_ref, hid, plain, xs, zs):
     for f in range(FIN + 1):
         plain[...] = perm_ref[0, plane] if f == FIN else feat_ref[0, f, plane].astype(F32)
         for y2 in range(2):
             xs[y2, pl.ds(f, PAIRS, stride=8), :] = plain[pl.ds(y2, PAIRS, stride=2), :]
     width = lo_ref.shape[1]
     parts = in_ref.shape[0] // width
-
-    def group(step, carry):
-        base = step * LIFT_UNROLL
-
-        def first(n):
-            u, r = n // parts, n % parts
-            start = pl.multiple_of((base + u) * ROWS * 8, ROWS * 8)
-            x = jnp.concatenate([xs[y2, pl.ds(start, ROWS * 8), :] for y2 in range(2)], 1)
-            return dot32(in_ref[r * width : (r + 1) * width, :], x.astype(BF))
-
-        now = first(0)
-        done = []
-        for n in range(LIFT_UNROLL * parts):
-            later = first(n + 1) if n + 1 < LIFT_UNROLL * parts else None
-            done.append(dot32(lo_ref[...], gelu_of_half(now)).astype(BF))
-            now = later
-            if len(done) == parts:
-                index = base + n // parts
-                hidden = jnp.concatenate(done, 0)
-                done = []
-                hid[plane, hid_rows(index), :] = hidden
-                lay_out(zs, index * ROWS, dot32(hidden, zf_ref[...]))
-        return carry
-
-    lax.fori_loop(0, PAIRS // ROWS // LIFT_UNROLL, group, 0)
-
-
-def from_modes(plane, count, recv, yi_ref, flat, zs):
+    total = PAIRS // ROWS * parts
+
+    def first(n):
+        u, r = n // parts, n % parts
+        x = jnp.concatenate([xs[y2, pl.ds(u * ROWS * 8, ROWS * 8), :] for y2 in range(2)], 1)
+        return dot32(in_ref[r * width : (r + 1) * width, :], x.astype(BF))
+
+    ahead = {n: first(n) for n in range(LOOK)}
+    raw = {}
+
+    def finish(n):
+        if n % parts == parts - 1:
+            u = n // parts
+            hidden = jnp.concatenate([raw.pop(u * parts + r) for r in range(parts)], 0)
+            hid[plane, hid_rows(u), :] = hidden.astype(BF)
+            lay_out(zs, u * ROWS, hidden)
+
+    for n in range(total):
+        if n + LOOK < total:
+            ahead[n + LOOK] = first(n + LOOK)
+        raw[n] = dot32(lo_ref[...], gelu_of_half(ahead.pop(n)))
+        if n >= LAG:
+            finish(n - LAG)
+    for n in range(total - LAG, total):
+        finish(n)
+
+
+def from_modes(plane, count, recv, yi_ref, zi_ref, flat, sp):
     tiles = C * MZ // LANES
     slots = 2 * MY // count * tiles
     for src in range(count):
         flat[pl.ds(src * (slots + SKEW), slots), :] = recv[plane, src].astype(F32)
-    rows = []
-    for s in range(2 * MY // count):
-        rows.append(
-            jnp.concatenate(
-                [flat[pl.ds(s * tiles + t, count, stride=slots + SKEW), :] for t in range(tiles)], 1
-            ).astype(BF)
-        )
-    back = dot32(yi_ref[...], jnp.concatenate(rows, 0))
-    for group in range(C // 4):
-        lanes = slice(group * LANES, (group + 1) * LANES)
-        four = [back[g * PAIRS : (g + 1) * PAIRS, lanes] for g in range(4)]
-        for r, piece in enumerate(swap_blocks(four)):
-            zs[(group * 4 + r) * PITCH : (group * 4 + r) * PITCH + PAIRS, :] = piece
-
-
-def layer_rows(plane, index, zs, hid, zi_ref, kp):
-    start = index * ROWS
-    parts = [zs[pl.ds(start + r, C, stride=PITCH), :].astype(BF) for r in range(ROWS)]
-    spectral = dot32(jnp.concatenate(parts, 0), zi_ref[...])
-    return gelu_of_half(spectral + dot32(kp, hid[plane, hid_rows(index), :]))
-
-
-def middle_plane(plane, kp, zi_ref, zf_ref, hid, zs, zs2):
-    def block(index, carry):
-        hidden = layer_rows(plane, index, zs, hid, zi_ref, kp)
-        hid[plane, hid_rows(index), :] = hidden
-        lay_out(zs2, index * ROWS, dot32(hidden, zf_ref[...]))
-        return carry
-
-    lax.fori_loop(0, PAIRS // ROWS, block, 0, unroll=UNROLL)
-
-
-def final_plane(plane, kp, zi_ref, di_ref, do_ref, perm_ref, hid, zs, st_ref, cond_ref):
-    def block(index, carry):
-        hidden = layer_rows(plane, index, zs, hid, zi_ref, kp)
-        both = dot32(do_ref[...], gelu_of_half(dot32(di_ref[...], hidden)))
+    for pair in range(tiles // 2):
+        rows = []
+        for s in range(2 * MY // count):
+            part = [
+                flat[pl.ds(s * tiles + pair * 2 + half, count, stride=slots + SKEW), :]
+                for half in range(2)
+            ]
+            rows.append(jnp.concatenate(part, 1))
+        back = dot32(yi_ref[...], jnp.concatenate(rows, 0).astype(BF)).astype(BF)
+        for half in range(2):
+            lanes = slice(half * LANES, (half + 1) * LANES)
+            for y2 in range(2):
+                left = [back[(y2 * 2 + p) * PAIRS : (y2 * 2 + p + 1) * PAIRS, lanes] for p in range(2)]
+                field = dot32(jnp.concatenate(left, 1), zi_ref[...])
+                for r in range(4):
+                    o = (pair * 2 + half) * 4 + r
+                    sp[y2, pl.ds(o, PAIRS, stride=C + SKEW), :] = field[:, r * NZ : (r + 1) * NZ]
+
+
+def field_rows(index, sp):
+    halves = []
+    for y2 in range(2):
+        rows = [sp[y2, pl.ds((index * ROWS + r) * (C + SKEW), C), :] for r in range(ROWS)]
+        halves.append(jnp.concatenate(rows, 0))
+    return jnp.concatenate(halves, 1)
+
+
+def middle_plane(plane, kp, hid, sp, zs):
+    total = PAIRS // ROWS
+
+    def local_term(index):
+        return dot32(kp[...], hid[plane, hid_rows(index), :])
+
+    ahead = {n: local_term(n) for n in range(MID)}
+    for n in range(total):
+        if n + MID < total:
+            ahead[n + MID] = local_term(n + MID)
+        hidden = gelu_of_half(ahead.pop(n) + field_rows(n, sp))
+        hid[plane, hid_rows(n), :] = hidden
+        lay_out(zs, n * ROWS, hidden.astype(F32))
+
+
+def final_plane(plane, kp, di_ref, do_ref, perm_ref, hid, sp, st_ref, cond_ref):
+    total = PAIRS // ROWS
+    width = di_ref.shape[1]
+    parts = di_ref.shape[0] // width
+
+    def local_term(index):
+        return dot32(kp[...], hid[plane, hid_rows(index), :])
+
+    def decode(n):
+        hidden = gelu_of_half(ahead.pop(n) + field_rows(n, sp))
+        return [dot32(di_ref[r * width : (r + 1) * width, :], hidden) for r in range(parts)]
+
+    ahead = {n: local_term(n) for n in range(MID)}
+    raw = {0: decode(0)}
+    for n in range(total):
+        if n + MID < total:
+            ahead[n + MID] = local_term(n + MID)
+        if n + 1 < total:
+            raw[n + 1] = decode(n + 1)
+        both = 0.0
+        for r, part in enumerate(raw.pop(n)):
+            both = both + dot32(do_ref[:, r * width : (r + 1) * width], gelu_of_half(part))
         for y2 in range(2):
             lanes = slice(y2 * NZ, (y2 + 1) * NZ)
-            where = pl.ds(index * ROWS * 2 + y2, ROWS, stride=2)
+            where = pl.ds(n * ROWS * 2 + y2, ROWS, stride=2)
             st_ref[0, 0, plane, where, :] = both[:ROWS, lanes]
             st_ref[0, 1, plane, where, :] = both[ROWS:, lanes]
-        return carry
-
-    lax.fori_loop(0, PAIRS // ROWS, block, 0, unroll=UNROLL)
     sat = jax.nn.sigmoid(st_ref[0, 1, plane])
     st_ref[0, 1, plane] = sat
     cond_ref[0, plane] = mobility_of(sat, perm_ref[0, plane])
@@ -540,7 +556,7 @@
 def whole_kernel(
     planes, count, feat_ref, perm_ref, lift_in, lift_out, point, dec_in, dec_out, zf_ref, zi_ref,
     yf_ref, yi_ref, xf_ref, xi_ref, w_hbm, st_ref, cond_ref,
-    hid, wbuf, send_f, recv_f, send_b, recv_b, flat, spec, rows, mixed, turned, zs, zs2, xs, plain,
+    hid, wbuf, send_f, recv_f, send_b, recv_b, flat, spec, rows, mixed, turned, zs, sp, xs, plain,
     in_ref, lo_ref, kp_ref, di_ref, do_ref, w_sem, sf_sem, rf_sem, sb_sem, rb_sem,
 ):
     me = lax.axis_index("space")
@@ -581,8 +597,8 @@
         lax.fori_loop(0, planes, run, 0)
 
     def lift(plane):
-        lift_plane(plane, feat_ref, perm_ref, in_ref, lo_ref, zf_ref, hid, plain, xs, zs)
-        to_modes(plane, count, yf_ref, zs, flat, send_f)
+        lift_plane(plane, feat_ref, perm_ref, in_ref, lo_ref, hid, plain, xs, zs)
+        to_modes(plane, count, zf_ref, yf_ref, zs, flat, send_f)
         send_plane(me, count, plane, send_f, recv_f, sf_sem, rf_sem)
 
     over(lift)
@@ -597,18 +613,17 @@
             fetch = pltpu.make_async_copy(w_hbm.at[layer + 1], wbuf, w_sem.at[layer + 1])
             fetch.start()
         over(lambda plane: send_plane(me, count, plane, send_b, recv_b, sb_sem, rb_sem))
+        kp = kp_ref.at[layer]
 
         def rest(plane):
             wait_plane(count, plane, recv_b, rb_sem)
-            from_modes(plane, count, recv_b, yi_ref, flat, zs)
+            from_modes(plane, count, recv_b, yi_ref, zi_ref, flat, sp)
             if layer + 1 < LAYERS:
-                middle_plane(plane, kp_ref[layer], zi_ref, zf_ref, hid, zs, zs2)
-                to_modes(plane, count, yf_ref, zs2, flat, send_f)
+                middle_plane(plane, kp, hid, sp, zs)
+                to_modes(plane, count, zf_ref, yf_ref, zs, flat, send_f)
                 send_plane(me, count, plane, send_f, recv_f, sf_sem, rf_sem)
             else:
-                final_plane(
-                    plane, kp_ref[layer], zi_ref, di_ref, do_ref, perm_ref, hid, zs, st_ref, cond_ref
-                )
+                final_plane(plane, kp, di_ref, do_ref, perm_ref, hid, sp, st_ref, cond_ref)
 
         over(rest)
         over(lambda plane: wait_plane(count, plane, send_b, sb_sem))
@@ -693,8 +708,8 @@
             pltpu.VMEM((modes // MODE_STEP, 2 * MX, MODE_STEP * C), F32),
             pltpu.VMEM((modes, MX * 2 * C), F32),
             pltpu.VMEM((2 * MX * (C + SKEW), LANES), F32),
-            pltpu.VMEM((C * PITCH, LANES), F32),
-            pltpu.VMEM((C * PITCH, LANES), F32),
+            pltpu.VMEM((2, C * PITCH, LANES), F32),
+            pltpu.VMEM((2, PAIRS * (C + SKEW), LANES), F32),
             pltpu.VMEM((2, PAIRS * 8, NZ), F32),
             pltpu.VMEM((NY, NZ), F32),
             pltpu.VMEM((ROWS * lift, ROWS * 8), BF),

time: 169 us -> 147 us (0.87)
  Pallas kernels: 153 us -> 131 us
    pallas_call x1, Pallas kernels: 153 us -> 131 us  [local_fast(): pl.pallas_call(lambda *refs: whole_kernel(planes, count, *refs), in_specs...]
where the time goes in v2:
time: 147 us; the launch traced here: 146 us
  Pallas kernels  131 us (89%)
  starting transfers between devices  5.26 us (4%)
  local copies, waits for them, and re-layouts  2.9 us (2%)
  waiting for transfers between devices  2.53 us (2%)
  matrix products  2.38 us (2%)
  other arithmetic  1.53 us (1%)
    pallas_call x1, Pallas kernels, local_fast(): pl.pallas_call(lambda *refs: whole_kernel(planes, count, *refs), in_specs...  131 us
    ppermute x1, starting transfers between devices, padded_2(): lax.ppermute(lax.slice_in_dim(block, block.shape[dim] - width, None, axis...  3.34 us
  transfers between devices with their start and end apart: 2, of which 1 were waited for; matrix products, arithmetic and copies ran while one was open for 0% of the time, Pallas kernels for 0%

profile of v2, /device:TPU:1, one launch (start us, length us, event | category | flops | bytes accessed | tf_op | source)
XLA Modules:
  0.0 146.3 jit_solution(1439128408892666702)
XLA Ops:
  0.6 130.9 %whole.1 = (f32[1,2,8,128,128]{4,3,2,1,0:T(8,128)}, f32[1,8,128,128]{3,2,1,0:T(8,128)}) custom-call(bf16[1,4,8,128,128]{4,3,2,1,0:T(8,128)(2,1)} %refs_0_.1, f32[1,8,128,128]{3,2,1,0:T(8,128)} %refs_1_.1, bf16[5,128]{1,0:T(8,128)(2,1)} %refs_2_.1, bf16[32,128]{1,0:T(8,128)(2,1)} %bitcast.48, bf16[2,32,32]{2,1,0:T(8,128)(2,1)} %refs_4_.1, ...), custom_call_target="tpu_custom_call" | custom-call | tf_op jit(solution)/shard_map/whole/pallas_call | solution.py:691
  131.5 0.0 copy-start
  131.5 1.1 convert_bitcast_fusion.4
  132.7 0.0 copy-start.1
  132.7 1.2 fusion.30
  133.9 0.0 copy-start.2
  134.0 3.3 %collective-permute-start = (bf16[1,2,1,128,128]{4,3,2,1,0:T(8,128)(2,1)S(1)}, bf16[1,2,1,128,128]{4,3,2,1,0:T(8,128)(2,1)S(1)}, u32[]{:S(2)}, u32[]{:S(2)}) collective-permute-start(bf16[1,2,1,128,128]{4,3,2,1,0:T(8,128)(2,1)S(1)} %get-tuple-element.16), channel_id=1, source_target_pairs={{0,1},{1,2},{2,3},{3,4},{4,5},{5,6},{6,7},{7,8},{8,9},{9,10},{10,1... | collective-permute-start | bytes 196616 | tf_op jit(solution)/shard_map/ppermute | solution.py:28
  137.3 1.9 %collective-permute-start.1 = (bf16[1,2,1,128,128]{4,3,2,1,0:T(8,128)(2,1)S(1)}, bf16[1,2,1,128,128]{4,3,2,1,0:T(8,128)(2,1)S(1)}, u32[]{:S(2)}, u32[]{:S(2)}) collective-permute-start(bf16[1,2,1,128,128]{4,3,2,1,0:T(8,128)(2,1)S(1)} %get-tuple-element.17), channel_id=1, source_target_pairs={{1,0},{2,1},{3,2},{4,3},{5,4},{6,5},{7,6},{8,7},{9,8},{10,9},{11,1... | collective-permute-start | bytes 196616 | tf_op jit(solution)/shard_map/ppermute | solution.py:31
  139.3 0.0 copy-done
  139.3 0.0 copy-done.1
  139.4 0.0 copy-done.2
  139.4 0.1 fusion.23
  139.5 0.0 copy-start.3
  139.5 0.2 fusion.31
  139.7 0.5 copy-done.3
  140.1 0.1 fusion.22
  140.2 0.1 broadcast_multiply_fusion
  140.3 0.1 maximum_bitcast_fusion
  140.4 0.0 collective-permute-done
  140.4 2.5 %collective-permute-done.1 = bf16[1,2,1,128,128]{4,3,2,1,0:T(8,128)(2,1)S(1)} collective-permute-done((bf16[1,2,1,128,128]{4,3,2,1,0:T(8,128)(2,1)S(1)}, bf16[1,2,1,128,128]{4,3,2,1,0:T(8,128)(2,1)S(1)}, u32[]{:S(2)}, u32[]{:S(2)}) %collective-permute-start.1) | collective-permute-done | bytes 65568 | tf_op jit(solution)/shard_map/ppermute | solution.py:31
  142.9 2.4 %fusion = f32[1,8,128,128]{3,2,1,0:T(8,128)} fusion(f32[1,8,128,128]{3,2,1,0:T(8,128)S(1)} %slice_bitcast_fusion, f32[1,7,128,128]{3,2,1,0:T(8,128)S(1)} %get-tuple-element.21, f32[1,1,128,128]{3,2,1,0:T(8,128)S(1)} %get-tuple-element.10, f32[1,1,128,128]{3,2,1,0:T(8,128)S(1)} %get-tuple-element.11, f32[1,7,128,128]{3,2,1,0:T(8,128)S(1)} %get-tuple-element.22, ...), kind=kOutput, calls=%fused_computation.9 | convolution fusion | flops 55709696 | bytes 3801216 | tf_op jit(solution)/shard_map/bwa,bwz->baz/dot_general | solution.py:133
  145.3 1.0 copy.29
  (5 shorter events, 0.1 us)
Async XLA Ops:
  131.5 7.7 %copy-start = (f32[1,8,128,128]{3,2,1,0:T(8,128)S(1)}, f32[1,8,128,128]{3,2,1,0:T(8,128)}, u32[]{:S(2)}) copy-start(f32[1,8,128,128]{3,2,1,0:T(8,128)} %get-tuple-element.5) | copy-start | bytes 1572868
  132.7 6.6 %copy-start.1 = (f32[1,2,8,128,128]{4,3,2,1,0:T(8,128)S(1)}, f32[1,2,8,128,128]{4,3,2,1,0:T(8,128)}, u32[]{:S(2)}) copy-start(f32[1,2,8,128,128]{4,3,2,1,0:T(8,128)} %get-tuple-element.25) | copy-start | bytes 3145732
  133.9 5.4 %copy-start.2 = (s32[1,32]{1,0:T(1,128)S(1)}, s32[1,32]{1,0:T(1,128)}, u32[]{:S(2)}) copy-start(s32[1,32]{1,0:T(1,128)} %param.18) | copy-start | bytes 388
  134.0 6.4 %collective-permute-start = (bf16[1,2,1,128,128]{4,3,2,1,0:T(8,128)(2,1)S(1)}, bf16[1,2,1,128,128]{4,3,2,1,0:T(8,128)(2,1)S(1)}, u32[]{:S(2)}, u32[]{:S(2)}) collective-permute-start(bf16[1,2,1,128,128]{4,3,2,1,0:T(8,128)(2,1)S(1)} %get-tuple-element.16), channel_id=1, source_target_pairs={{0,1},{1,2},{2,3},{3,4},{4,5},{5,6},{6,7},{7,8},{8,9},{9,10},{10,1... | collective-permute-start | bytes 196616 | tf_op jit(solution)/shard_map/ppermute | solution.py:28
  137.3 5.6 %collective-permute-start.1 = (bf16[1,2,1,128,128]{4,3,2,1,0:T(8,128)(2,1)S(1)}, bf16[1,2,1,128,128]{4,3,2,1,0:T(8,128)(2,1)S(1)}, u32[]{:S(2)}, u32[]{:S(2)}) collective-permute-start(bf16[1,2,1,128,128]{4,3,2,1,0:T(8,128)(2,1)S(1)} %get-tuple-element.17), channel_id=1, source_target_pairs={{1,0},{2,1},{3,2},{4,3},{5,4},{6,5},{7,6},{8,7},{9,8},{10,9},{11,1... | collective-permute-start | bytes 196616 | tf_op jit(solution)/shard_map/ppermute | solution.py:31
  139.5 0.7 copy-start.3

commit v3 on v2

--- a/solution.py
+++ b/solution.py
@@ -220,7 +220,9 @@
 ROWS = 8
 LOOK = 4
 LAG = 1
-MID = 2
+MID = 3
+TB = 2
+FB = 4
 LANES = 128
 
 
@@ -303,14 +305,24 @@
 def to_modes(plane, count, zf_ref, yf_ref, zs, flat, send):
     tiles = C * MZ // LANES
     slots = 2 * MY // count * tiles
+    halves = {}
+    for first in range(0, tiles, 2 * TB):
+        some = [(group, y2) for group in range(first, first + 2 * TB) for y2 in range(2)]
+        left = [
+            jnp.concatenate(
+                [zs[y2, pl.ds((group * 4 + r) * PITCH, PAIRS), :] for r in range(4)], 1
+            ).astype(BF)
+            for group, y2 in some
+        ]
+        waves = dot32(jnp.concatenate(left, 0), zf_ref[...]).astype(BF)
+        for n, key in enumerate(some):
+            halves[key] = waves[n * PAIRS : (n + 1) * PAIRS, :]
     for pair in range(tiles // 2):
         columns = []
         for group in (pair * 2, pair * 2 + 1):
-            halves = []
-            for y2 in range(2):
-                left = [zs[y2, pl.ds((group * 4 + r) * PITCH, PAIRS), :] for r in range(4)]
-                halves.append(dot32(jnp.concatenate(left, 1).astype(BF), zf_ref[...]).astype(BF))
-            parts = [half[:, p * LANES : (p + 1) * LANES] for half in halves for p in range(2)]
+            parts = [
+                halves[group, y2][:, p * LANES : (p + 1) * LANES] for y2 in range(2) for p in range(2)
+            ]
             columns.append(jnp.concatenate(parts, 0))
         modes = dot32(yf_ref[...], jnp.concatenate(columns, 1))
         for s in range(2 * MY // count):
@@ -373,7 +385,8 @@
     slots = 2 * MY // count * tiles
     for src in range(count):
         flat[pl.ds(src * (slots + SKEW), slots), :] = recv[plane, src].astype(F32)
-    for pair in range(tiles // 2):
+
+    def back_of(pair):
         rows = []
         for s in range(2 * MY // count):
             part = [
@@ -381,15 +394,26 @@
                 for half in range(2)
             ]
             rows.append(jnp.concatenate(part, 1))
-        back = dot32(yi_ref[...], jnp.concatenate(rows, 0).astype(BF)).astype(BF)
-        for half in range(2):
-            lanes = slice(half * LANES, (half + 1) * LANES)
-            for y2 in range(2):
-                left = [back[(y2 * 2 + p) * PAIRS : (y2 * 2 + p + 1) * PAIRS, lanes] for p in range(2)]
-                field = dot32(jnp.concatenate(left, 1), zi_ref[...])
-                for r in range(4):
-                    o = (pair * 2 + half) * 4 + r
-                    sp[y2, pl.ds(o, PAIRS, stride=C + SKEW), :] = field[:, r * NZ : (r + 1) * NZ]
+        return dot32(yi_ref[...], jnp.concatenate(rows, 0).astype(BF)).astype(BF)
+
+    for first in range(0, tiles // 2, FB):
+        left, some = [], []
+        for pair in range(first, first + FB):
+            back = back_of(pair)
+            for half in range(2):
+                lanes = slice(half * LANES, (half + 1) * LANES)
+                for y2 in range(2):
+                    parts = [
+                        back[(y2 * 2 + p) * PAIRS : (y2 * 2 + p + 1) * PAIRS, lanes] for p in range(2)
+                    ]
+                    left.append(jnp.concatenate(parts, 1))
+                    some.append(((pair * 2 + half) * 4, y2))
+        field = dot32(jnp.concatenate(left, 0), zi_ref[...])
+        for n, (o, y2) in enumerate(some):
+            for r in range(4):
+                sp[y2, pl.ds(o + r, PAIRS, stride=C + SKEW), :] = field[
+                    n * PAIRS : (n + 1) * PAIRS, r * NZ : (r + 1) * NZ
+                ]
 
 
 def field_rows(index, sp):
@@ -423,20 +447,31 @@
     def local_term(index):
         return dot32(kp[...], hid[plane, hid_rows(index), :])
 
-    def decode(n):
-        hidden = gelu_of_half(ahead.pop(n) + field_rows(n, sp))
-        return [dot32(di_ref[r * width : (r + 1) * width, :], hidden) for r in range(parts)]
+    def mixed(n):
+        return gelu_of_half(ahead.pop(n) + field_rows(n, sp))
+
+    def decode(hidden, r):
+        return dot32(di_ref[r * width : (r + 1) * width, :], hidden)
+
+    def shrink(n, r):
+        return dot32(do_ref[:, r * width : (r + 1) * width], gelu_of_half(raw.pop((n, r))))
 
     ahead = {n: local_term(n) for n in range(MID)}
-    raw = {0: decode(0)}
+    raw = {}
+    hiddens = {0: mixed(0)}
+    for r in range(parts):
+        raw[0, r] = decode(hiddens[0], r)
+    hiddens[1] = mixed(1)
     for n in range(total):
         if n + MID < total:
             ahead[n + MID] = local_term(n + MID)
-        if n + 1 < total:
-            raw[n + 1] = decode(n + 1)
         both = 0.0
-        for r, part in enumerate(raw.pop(n)):
-            both = both + dot32(do_ref[:, r * width : (r + 1) * width], gelu_of_half(part))
+        for r in range(parts):
+            if n + 1 < total:
+                raw[n + 1, r] = decode(hiddens[n + 1], r)
+            both = both + shrink(n, r)
+            if r == 0 and n + 2 < total:
+                hiddens[n + 2] = mixed(n + 2)
         for y2 in range(2):
             lanes = slice(y2 * NZ, (y2 + 1) * NZ)
             where = pl.ds(n * ROWS * 2 + y2, ROWS, stride=2)

time: 147 us -> 138 us (0.939)
  Pallas kernels: 131 us -> 122 us
    pallas_call x1, Pallas kernels: 131 us -> 122 us  [local_fast(): pl.pallas_call(lambda *refs: whole_kernel(planes, count, *refs), in_specs...]
where the time goes in v3:
time: 138 us
  Pallas kernels  122 us (88%)
  starting transfers between devices  5.26 us (4%)
  local copies, waits for them, and re-layouts  2.9 us (2%)
  waiting for transfers between devices  2.53 us (2%)
  matrix products  2.38 us (2%)
  other arithmetic  1.53 us (1%)
    pallas_call x1, Pallas kernels, local_fast(): pl.pallas_call(lambda *refs: whole_kernel(planes, count, *refs), in_specs...  122 us
    ppermute x1, starting transfers between devices, padded_2(): lax.ppermute(lax.slice_in_dim(block, block.shape[dim] - width, None, axis...  3.34 us
  transfers between devices with their start and end apart: 2, of which 1 were waited for; matrix products, arithmetic and copies ran while one was open for 0% of the time, Pallas kernels for 0%

profile of v3, /device:TPU:1, one launch (start us, length us, event | category | flops | bytes accessed | tf_op | source)
XLA Modules:
  0.0 137.7 jit_solution(17024928387651238465)
XLA Ops:
  0.6 122.3 %whole.1 = (f32[1,2,8,128,128]{4,3,2,1,0:T(8,128)}, f32[1,8,128,128]{3,2,1,0:T(8,128)}) custom-call(bf16[1,4,8,128,128]{4,3,2,1,0:T(8,128)(2,1)} %refs_0_.1, f32[1,8,128,128]{3,2,1,0:T(8,128)} %refs_1_.1, bf16[5,128]{1,0:T(8,128)(2,1)} %refs_2_.1, bf16[32,128]{1,0:T(8,128)(2,1)} %bitcast.48, bf16[2,32,32]{2,1,0:T(8,128)(2,1)} %refs_4_.1, ...), custom_call_target="tpu_custom_call" | custom-call | tf_op jit(solution)/shard_map/whole/pallas_call | solution.py:726
  122.9 0.0 copy-start
  123.0 1.1 convert_bitcast_fusion.4
  124.1 0.0 copy-start.1
  124.1 1.2 fusion.30
  125.3 0.0 copy-start.2
  125.4 3.3 %collective-permute-start = (bf16[1,2,1,128,128]{4,3,2,1,0:T(8,128)(2,1)S(1)}, bf16[1,2,1,128,128]{4,3,2,1,0:T(8,128)(2,1)S(1)}, u32[]{:S(2)}, u32[]{:S(2)}) collective-permute-start(bf16[1,2,1,128,128]{4,3,2,1,0:T(8,128)(2,1)S(1)} %get-tuple-element.16), channel_id=1, source_target_pairs={{0,1},{1,2},{2,3},{3,4},{4,5},{5,6},{6,7},{7,8},{8,9},{9,10},{10,1... | collective-permute-start | bytes 196616 | tf_op jit(solution)/shard_map/ppermute | solution.py:28
  128.7 1.9 %collective-permute-start.1 = (bf16[1,2,1,128,128]{4,3,2,1,0:T(8,128)(2,1)S(1)}, bf16[1,2,1,128,128]{4,3,2,1,0:T(8,128)(2,1)S(1)}, u32[]{:S(2)}, u32[]{:S(2)}) collective-permute-start(bf16[1,2,1,128,128]{4,3,2,1,0:T(8,128)(2,1)S(1)} %get-tuple-element.17), channel_id=1, source_target_pairs={{1,0},{2,1},{3,2},{4,3},{5,4},{6,5},{7,6},{8,7},{9,8},{10,9},{11,1... | collective-permute-start | bytes 196616 | tf_op jit(solution)/shard_map/ppermute | solution.py:31
  130.7 0.0 copy-done
  130.7 0.0 copy-done.1
  130.8 0.0 copy-done.2
  130.8 0.1 fusion.23
  130.9 0.0 copy-start.3
  130.9 0.2 fusion.31
  131.1 0.5 copy-done.3
  131.5 0.1 fusion.22
  131.6 0.1 broadcast_multiply_fusion
  131.7 0.1 maximum_bitcast_fusion
  131.8 0.0 collective-permute-done
  131.8 2.5 %collective-permute-done.1 = bf16[1,2,1,128,128]{4,3,2,1,0:T(8,128)(2,1)S(1)} collective-permute-done((bf16[1,2,1,128,128]{4,3,2,1,0:T(8,128)(2,1)S(1)}, bf16[1,2,1,128,128]{4,3,2,1,0:T(8,128)(2,1)S(1)}, u32[]{:S(2)}, u32[]{:S(2)}) %collective-permute-start.1) | collective-permute-done | bytes 65568 | tf_op jit(solution)/shard_map/ppermute | solution.py:31
  134.3 2.4 %fusion = f32[1,8,128,128]{3,2,1,0:T(8,128)} fusion(f32[1,8,128,128]{3,2,1,0:T(8,128)S(1)} %slice_bitcast_fusion, f32[1,7,128,128]{3,2,1,0:T(8,128)S(1)} %get-tuple-element.21, f32[1,1,128,128]{3,2,1,0:T(8,128)S(1)} %get-tuple-element.10, f32[1,1,128,128]{3,2,1,0:T(8,128)S(1)} %get-tuple-element.11, f32[1,7,128,128]{3,2,1,0:T(8,128)S(1)} %get-tuple-element.22, ...), kind=kOutput, calls=%fused_computation.9 | convolution fusion | flops 55709696 | bytes 3801216 | tf_op jit(solution)/shard_map/bwa,bwz->baz/dot_general | solution.py:133
  136.7 1.0 copy.29
  (5 shorter events, 0.1 us)
Async XLA Ops:
  122.9 7.7 %copy-start = (f32[1,8,128,128]{3,2,1,0:T(8,128)S(1)}, f32[1,8,128,128]{3,2,1,0:T(8,128)}, u32[]{:S(2)}) copy-start(f32[1,8,128,128]{3,2,1,0:T(8,128)} %get-tuple-element.5) | copy-start | bytes 1572868
  124.1 6.6 %copy-start.1 = (f32[1,2,8,128,128]{4,3,2,1,0:T(8,128)S(1)}, f32[1,2,8,128,128]{4,3,2,1,0:T(8,128)}, u32[]{:S(2)}) copy-start(f32[1,2,8,128,128]{4,3,2,1,0:T(8,128)} %get-tuple-element.25) | copy-start | bytes 3145732
  125.3 5.4 %copy-start.2 = (s32[1,32]{1,0:T(1,128)S(1)}, s32[1,32]{1,0:T(1,128)}, u32[]{:S(2)}) copy-start(s32[1,32]{1,0:T(1,128)} %param.18) | copy-start | bytes 388
  125.4 6.4 %collective-permute-start = (bf16[1,2,1,128,128]{4,3,2,1,0:T(8,128)(2,1)S(1)}, bf16[1,2,1,128,128]{4,3,2,1,0:T(8,128)(2,1)S(1)}, u32[]{:S(2)}, u32[]{:S(2)}) collective-permute-start(bf16[1,2,1,128,128]{4,3,2,1,0:T(8,128)(2,1)S(1)} %get-tuple-element.16), channel_id=1, source_target_pairs={{0,1},{1,2},{2,3},{3,4},{4,5},{5,6},{6,7},{7,8},{8,9},{9,10},{10,1... | collective-permute-start | bytes 196616 | tf_op jit(solution)/shard_map/ppermute | solution.py:28
  128.7 5.6 %collective-permute-start.1 = (bf16[1,2,1,128,128]{4,3,2,1,0:T(8,128)(2,1)S(1)}, bf16[1,2,1,128,128]{4,3,2,1,0:T(8,128)(2,1)S(1)}, u32[]{:S(2)}, u32[]{:S(2)}) collective-permute-start(bf16[1,2,1,128,128]{4,3,2,1,0:T(8,128)(2,1)S(1)} %get-tuple-element.17), channel_id=1, source_target_pairs={{1,0},{2,1},{3,2},{4,3},{5,4},{6,5},{7,6},{8,7},{9,8},{10,9},{11,1... | collective-permute-start | bytes 196616 | tf_op jit(solution)/shard_map/ppermute | solution.py:31
  130.9 0.7 copy-start.3

commit v4 on v3

--- a/solution.py
+++ b/solution.py
@@ -439,7 +439,7 @@
         lay_out(zs, n * ROWS, hidden.astype(F32))
 
 
-def final_plane(plane, kp, di_ref, do_ref, perm_ref, hid, sp, st_ref, cond_ref):
+def final_plane(plane, kp, di_ref, do_ref, perm_ref, hid, sp, st_ref):
     total = PAIRS // ROWS
     width = di_ref.shape[1]
     parts = di_ref.shape[0] // width
@@ -477,9 +477,59 @@
             where = pl.ds(n * ROWS * 2 + y2, ROWS, stride=2)
             st_ref[0, 0, plane, where, :] = both[:ROWS, lanes]
             st_ref[0, 1, plane, where, :] = both[ROWS:, lanes]
+
+def residual_plane(plane, me, planes, perm_ref, cells, rates, ends, st_ref, res_ref, cond):
     sat = jax.nn.sigmoid(st_ref[0, 1, plane])
     st_ref[0, 1, plane] = sat
-    cond_ref[0, plane] = mobility_of(sat, perm_ref[0, plane])
+    conduct = mobility_of(sat, perm_ref[0, plane])
+    cond[plane] = conduct
+    pressure = st_ref[0, 0, plane]
+    flux = 0.0
+    for axis in range(2):
+        length = pressure.shape[axis]
+        inner = lax.broadcasted_iota(jnp.int32, pressure.shape, axis) < length - 1
+        beyond = (pltpu.roll(field, length - 1, axis) for field in (conduct, pressure))
+        cond_next, press_next = beyond
+        face = jnp.where(inner, face_term(conduct, cond_next, pressure, press_next), 0.0)
+        flux = flux + face - pltpu.roll(face, 1, axis)
+    shape = (NY, cells.shape[1])
+    here = cells[...] - (me * planes + plane) * (NY * NZ)
+    starts = lax.broadcasted_iota(jnp.int32, shape, 0) * NZ
+    offset = here - starts
+    hit = (offset >= 0) & (offset < NZ)
+    left = jnp.where(hit, rates[...], 0.0).astype(BF)
+    dims = (((1,), (1,)), ((), ()))
+    source = lax.dot_general(left, ends[...], dims, preferred_element_type=F32)
+    res_ref[0, plane] = flux - source
+
+
+def add_face(plane, st_ref, res_ref, cond):
+    face = face_term(cond[plane], cond[plane + 1], st_ref[0, 0, plane], st_ref[0, 0, plane + 1])
+    res_ref[0, plane] = res_ref[0, plane] + face
+    res_ref[0, plane + 1] = res_ref[0, plane + 1] - face
+
+
+def edge_copy(me, count, side, edge_send, edge_recv, es_sem, er_sem):
+    return pltpu.make_async_remote_copy(
+        src_ref=edge_send.at[side],
+        dst_ref=edge_recv.at[1 - side],
+        send_sem=es_sem.at[side],
+        recv_sem=er_sem.at[1 - side],
+        device_id={"space": lax.rem(me + (1 if side else count - 1), count)},
+        device_id_type=pl.DeviceIdType.MESH,
+    )
+
+
+def wells_of(cells_ref, rates_ref, cells, rates, ends):
+    rate = rates_ref[...]
+    high = rate.astype(BF).astype(F32)
+    middle = (rate - high).astype(BF).astype(F32)
+    for n, part in enumerate((high, middle, rate - high - middle)):
+        lanes = slice(n * WELLS, (n + 1) * WELLS)
+        cells[:, lanes] = cells_ref[...]
+        rates[:, lanes] = part
+    column = lax.broadcasted_iota(jnp.int32, ends.shape, 0)
+    ends[...] = jnp.where((cells[...] & (NZ - 1)) == column, 1.0, 0.0).astype(BF)
 
 
 def mix_modes(planes, count, recv, send, wbuf, xf_ref, xi_ref, flat, spec, rows, mixed, turned):
@@ -590,9 +640,10 @@
 
 def whole_kernel(
     planes, count, feat_ref, perm_ref, lift_in, lift_out, point, dec_in, dec_out, zf_ref, zi_ref,
-    yf_ref, yi_ref, xf_ref, xi_ref, w_hbm, st_ref, cond_ref,
+    yf_ref, yi_ref, xf_ref, xi_ref, cells_ref, rates_ref, w_hbm, st_ref, res_ref,
     hid, wbuf, send_f, recv_f, send_b, recv_b, flat, spec, rows, mixed, turned, zs, sp, xs, plain,
-    in_ref, lo_ref, kp_ref, di_ref, do_ref, w_sem, sf_sem, rf_sem, sb_sem, rb_sem,
+    in_ref, lo_ref, kp_ref, di_ref, do_ref, cond, cells, rates, ends, edge_send, edge_recv,
+    w_sem, sf_sem, rf_sem, sb_sem, rb_sem, es_sem, er_sem,
 ):
     me = lax.axis_index("space")
     barrier = pltpu.get_barrier_semaphore()
@@ -622,6 +673,7 @@
         1.0,
         True,
     )
+    wells_of(cells_ref, rates_ref, cells, rates, ends)
     pl.semaphore_wait(barrier, count - 1)
 
     def over(body):
@@ -647,21 +699,50 @@
         if layer + 1 < LAYERS:
             fetch = pltpu.make_async_copy(w_hbm.at[layer + 1], wbuf, w_sem.at[layer + 1])
             fetch.start()
-        over(lambda plane: send_plane(me, count, plane, send_b, recv_b, sb_sem, rb_sem))
+        last = layer + 1 == LAYERS
+
+        def turn(index):
+            return lax.rem(planes - index, planes) if last else index
+
+        over(lambda n: send_plane(me, count, turn(n), send_b, recv_b, sb_sem, rb_sem))
         kp = kp_ref.at[layer]
 
-        def rest(plane):
+        def rest(index):
+            plane = turn(index)
             wait_plane(count, plane, recv_b, rb_sem)
             from_modes(plane, count, recv_b, yi_ref, zi_ref, flat, sp)
-            if layer + 1 < LAYERS:
+            if not last:
                 middle_plane(plane, kp, hid, sp, zs)
                 to_modes(plane, count, zf_ref, yf_ref, zs, flat, send_f)
                 send_plane(me, count, plane, send_f, recv_f, sf_sem, rf_sem)
             else:
-                final_plane(plane, kp, di_ref, do_ref, perm_ref, hid, sp, st_ref, cond_ref)
+                final_plane(plane, kp, di_ref, do_ref, perm_ref, hid, sp, st_ref)
+                residual_plane(
+                    plane, me, planes, perm_ref, cells, rates, ends, st_ref, res_ref, cond
+                )
+
+                @pl.when(index == 1)
+                def _():
+                    for side in range(2):
+                        edge_send[side, 0] = st_ref[0, 0, side * (planes - 1)].astype(BF)
+                        edge_send[side, 1] = cond[side * (planes - 1)].astype(BF)
+                        edge_copy(me, count, side, edge_send, edge_recv, es_sem, er_sem).start()
+
+                @pl.when(index >= 2)
+                def _():
+                    add_face(plane, st_ref, res_ref, cond)
 
         over(rest)
         over(lambda plane: wait_plane(count, plane, send_b, sb_sem))
+    add_face(0, st_ref, res_ref, cond)
+    for side in range(2):
+        edge_copy(me, count, side, edge_send, edge_recv, es_sem, er_sem).wait()
+    for side in range(2):
+        plane = side * (planes - 1)
+        press, conduct = (edge_recv[side, n].astype(F32) for n in range(2))
+        face = face_term(cond[plane], conduct, st_ref[0, 0, plane], press)
+        inside = me < count - 1 if side else me > 0
+        res_ref[0, plane] = res_ref[0, plane] + jnp.where(inside, face, 0.0)
 
 
 def ones_where(shape, test, value=1.0):
@@ -721,9 +802,10 @@
         dec_in,
         dec_out.T,
     ) + tuple(tables[name] for name in ("zf", "zi", "yf", "yi", "xf", "xi"))
+    operands = operands + (well_cells, well_rates)
     vmem = pl.BlockSpec(memory_space=pltpu.VMEM)
     exchange = pltpu.VMEM((planes, count, slots, LANES), BF)
-    states, conduct = pl.pallas_call(
+    return pl.pallas_call(
         lambda *refs: whole_kernel(planes, count, *refs),
         in_specs=[vmem] * len(operands) + [pl.BlockSpec(memory_space=pl.ANY)],
         out_specs=[vmem, vmem],
@@ -752,15 +834,21 @@
             pltpu.VMEM((LAYERS, ROWS * C, ROWS * C), BF),
             pltpu.VMEM((ROWS * dec, ROWS * C), BF),
             pltpu.VMEM((2 * ROWS, ROWS * dec), BF),
+            pltpu.VMEM((planes, NY, NZ), F32),
+            pltpu.VMEM((1, 3 * WELLS), jnp.int32),
+            pltpu.VMEM((1, 3 * WELLS), F32),
+            pltpu.VMEM((NZ, 3 * WELLS), BF),
+            pltpu.VMEM((2, 2, NY, NZ), BF),
+            pltpu.VMEM((2, 2, NY, NZ), BF),
             pltpu.SemaphoreType.DMA((LAYERS,)),
         ]
-        + [pltpu.SemaphoreType.DMA((planes,))] * 4,
+        + [pltpu.SemaphoreType.DMA((planes,))] * 4
+        + [pltpu.SemaphoreType.DMA((2,))] * 2,
         compiler_params=pltpu.CompilerParams(
             collective_id=0, has_side_effects=True, vmem_limit_bytes=60 * 1024 * 1024
         ),
         name="whole",
     )(*operands, spec_weight)
-    return (states, darcy(states[:, 0], conduct, well_cells, well_rates))
 
 
 def local(features, log_perm, well_cells, well_rates, lift_in, lift_out, spec_weight, *rest):

time: 138 us -> 129 us (0.935)
  starting transfers between devices: 5.26 us -> 0 us
  waiting for transfers between devices: 2.53 us -> 0 us
  matrix products: 2.38 us -> 0 us
  other arithmetic: 1.53 us -> 0 us
    ppermute x2 -> x0, starting transfers between devices: 5.26 us -> none  [the longest x1 3.34 us: padded_2(): lax.ppermute(lax.slice_in_dim(block, block.shape[dim] - width, None, axis...]
    unnamed x9 -> x2, local copies, waits for them, and re-layouts: 1.44 us -> 4.17 us
    ppermute x2 -> x0, waiting for transfers between devices: 2.53 us -> none  [the longest x1 2.53 us: padded_2(): lax.ppermute(lax.slice_in_dim(block, 0, width, axis=dim), axis, backward)]
    dot_general x1 -> x0, matrix products: 2.38 us -> none  [darcy(): jnp.einsum('bwa,bwz->baz', plane_rows, onehot_z, precision=lax.Precision....]
  transfers between devices with their start and end apart: 2 -> 0, of which waited for: 1 -> 0; matrix products, arithmetic and copies ran while one was open for 0% -> 0% of each run, Pallas kernels for 0% -> 0%
where the time goes in v4:
time: 129 us; the launch traced here: 128 us
  Pallas kernels  123 us (95%)
  local copies, waits for them, and re-layouts  4.17 us (3%)
    pallas_call x1, Pallas kernels, local_fast(): pl.pallas_call(lambda *refs: whole_kernel(planes, count, *refs), in_specs...  123 us
    unnamed x2, local copies, waits for them, and re-layouts  4.17 us

profile of v4, /device:TPU:1, one launch (start us, length us, event | category | flops | bytes accessed | tf_op | source)
XLA Modules:
  0.0 128.2 jit_solution(3300933558484314431)
XLA Ops:
  0.6 123.4 %whole.1 = (f32[1,2,8,128,128]{4,3,2,1,0:T(8,128)}, f32[1,8,128,128]{3,2,1,0:T(8,128)}) custom-call(bf16[1,4,8,128,128]{4,3,2,1,0:T(8,128)(2,1)} %refs_0_.1, f32[1,8,128,128]{3,2,1,0:T(8,128)} %refs_1_.1, bf16[5,128]{1,0:T(8,128)(2,1)} %refs_2_.1, bf16[32,128]{1,0:T(8,128)(2,1)} %bitcast.2, bf16[2,32,32]{2,1,0:T(8,128)(2,1)} %refs_4_.1, ...), custom_call_target="tpu_custom_call" | custom-call | tf_op jit(solution)/shard_map/whole/pallas_call | solution.py:808
  124.0 2.3 %copy.20 = f32[1,2,8,128,128]{4,3,2,1,0:T(8,128)} copy(f32[1,2,8,128,128]{4,3,2,1,0:T(8,128)} %get-tuple-element.4) | data formatting | bytes 2097152
  126.3 1.9 %copy.21 = f32[1,8,128,128]{3,2,1,0:T(8,128)} copy(f32[1,8,128,128]{3,2,1,0:T(8,128)} %get-tuple-element.5) | data formatting | bytes 1048576

commit v5 on v4

--- a/solution.py
+++ b/solution.py
@@ -269,6 +269,8 @@
         "xf": by_plane(np_forward(NX, MX).transpose(2, 3, 1, 0), 3, count).reshape(2 * MX, 2 * NX),
         "xi": by_plane(np_inverse(NX, MX).transpose(2, 3, 0, 1), 1, count).reshape(2 * NX, 2 * MX),
     }
+    halves = tables["xi"].reshape(2, NX // count, 2, count // 2, 2 * MX)
+    tables["xh"] = halves.transpose(2, 0, 1, 3, 4).reshape(2, NX, 2 * MX)
     return {name: jnp.asarray(table.astype(np.float32)).astype(BF) for name, table in tables.items()}
 
 
@@ -297,8 +299,8 @@
     recv[plane, me] = send[plane, me]
 
 
-def wait_plane(count, plane, buffer, sem):
-    part = buffer.at[plane, pl.ds(0, count - 1)]
+def wait_plane(parts, plane, buffer, sem):
+    part = buffer.at[plane, pl.ds(0, parts)]
     pltpu.make_async_copy(part, part, sem.at[plane]).wait()
 
 
@@ -532,7 +534,7 @@
     ends[...] = jnp.where((cells[...] & (NZ - 1)) == column, 1.0, 0.0).astype(BF)
 
 
-def mix_modes(planes, count, recv, send, wbuf, xf_ref, xi_ref, flat, spec, rows, mixed, turned):
+def mix_modes(planes, count, recv, wbuf, xf_ref, flat, spec, rows, mixed, turned):
     own = MY // count
     tiles = C * MZ // LANES
     slots = 2 * own * tiles
@@ -611,39 +613,84 @@
         for r in range(4):
             first = (block * 4 + r) * (C + SKEW)
             turned[pl.ds(first, C), : own * MZ] = part[r * C : (r + 1) * C, :]
-    for pair in range(tiles // 2):
-        right = [[], []]
+
+
+def mixed_tile(pair, turned):
+    lane = lax.broadcasted_iota(jnp.int32, (1, LANES), 1)
+    low = lane < 64
+    even = lane % 64 < 32
+    right = [[], []]
+    for half in range(2):
+        o = (pair * 2 + half) * 4
+        a = [turned[pl.ds(o + r, 2 * MX, stride=C + SKEW), :] for r in range(4)]
+        b = jnp.where(low, a[0], pltpu.roll(a[2], 64, 1))
+        c = jnp.where(low, a[1], pltpu.roll(a[3], 64, 1))
+        right[0].append(jnp.where(even, b, pltpu.roll(c, 32, 1)))
+        right[1].append(jnp.where(even, pltpu.roll(b, LANES - 32, 1), c))
+    return [jnp.concatenate(part, 1).astype(BF) for part in right]
+
+
+def to_planes(table, tile, jj, pair, count, flat):
+    own = MY // count
+    tiles = C * MZ // LANES
+    pitch = 2 * own * tiles + SKEW
+    back = dot32(table, tile)
+    every = back.shape[0] // 2
+    for p in range(2):
         for half in range(2):
-            o = (pair * 2 + half) * 4
-            a = [turned[pl.ds(o + r, 2 * MX, stride=C + SKEW), :] for r in range(4)]
-            b = jnp.where(low, a[0], pltpu.roll(a[2], 64, 1))
-            c = jnp.where(low, a[1], pltpu.roll(a[3], 64, 1))
-            right[0].append(jnp.where(even, b, pltpu.roll(c, 32, 1)))
-            right[1].append(jnp.where(even, pltpu.roll(b, LANES - 32, 1), c))
-        for jj in range(own):
-            back = dot32(xi_ref[...], jnp.concatenate(right[jj], 1).astype(BF))
-            for p in range(2):
-                for half in range(2):
-                    slot = (p * own + jj) * tiles + pair * 2 + half
-                    flat[pl.ds(slot, every, stride=pitch), :] = back[
-                        p * every : (p + 1) * every, half * LANES : (half + 1) * LANES
-                    ]
+            slot = (p * own + jj) * tiles + pair * 2 + half
+            flat[pl.ds(slot, every, stride=pitch), :] = back[
+                p * every : (p + 1) * every, half * LANES : (half + 1) * LANES
+            ]
+
+
+def pack_planes(planes, count, first, targets, flat, send):
+    slots = 2 * MY // count * C * MZ // LANES
+    pitch = slots + SKEW
 
     def pack(plane, carry):
-        for dst in range(count):
-            start = (plane * count + dst) * pitch
-            send[plane, dst] = flat[pl.ds(start, slots), :].astype(BF)
+        for dst in range(targets):
+            start = (plane * targets + dst) * pitch
+            send[plane, first + dst] = flat[pl.ds(start, slots), :].astype(BF)
         return carry
 
     lax.fori_loop(0, planes, pack, 0)
+
+
+def send_half(me, count, plane, other, send, recv, send_sem, recv_sem):
+    near = count // 2
+    owner = lax.rem(me + other * near, count)
+    for shift in range(1, near):
+        place = lax.rem(me + shift, near)
+        pltpu.make_async_remote_copy(
+            src_ref=send.at[plane, other * near + place],
+            dst_ref=recv.at[plane, owner],
+            send_sem=send_sem.at[plane],
+            recv_sem=recv_sem.at[plane],
+            device_id={"space": me // near * near + place},
+            device_id_type=pl.DeviceIdType.MESH,
+        ).start()
+    recv[plane, owner] = send[plane, other * near + lax.rem(me, near)]
+
+
+def swap_tile(me, count, n, own, other, send_sem, recv_sem):
+    return pltpu.make_async_remote_copy(
+        src_ref=own.at[n],
+        dst_ref=other.at[n],
+        send_sem=send_sem.at[n],
+        recv_sem=recv_sem.at[n],
+        device_id={"space": lax.rem(me + count // 2, count)},
+        device_id_type=pl.DeviceIdType.MESH,
+    )
 
 
 def whole_kernel(
     planes, count, feat_ref, perm_ref, lift_in, lift_out, point, dec_in, dec_out, zf_ref, zi_ref,
-    yf_ref, yi_ref, xf_ref, xi_ref, cells_ref, rates_ref, w_hbm, st_ref, res_ref,
+    yf_ref, yi_ref, xf_ref, xi_ref, xh_ref, cells_ref, rates_ref, w_hbm, st_ref, res_ref,
     hid, wbuf, send_f, recv_f, send_b, recv_b, flat, spec, rows, mixed, turned, zs, sp, xs, plain,
     in_ref, lo_ref, kp_ref, di_ref, do_ref, cond, cells, rates, ends, edge_send, edge_recv,
-    w_sem, sf_sem, rf_sem, sb_sem, rb_sem, es_sem, er_sem,
+    own_mixed, other_mixed,
+    w_sem, sf_sem, rf_sem, sb_sem, rb_sem, es_sem, er_sem, om_sem, rm_sem,
 ):
     me = lax.axis_index("space")
     barrier = pltpu.get_barrier_semaphore()
@@ -691,11 +738,9 @@
     over(lift)
     for layer in range(LAYERS):
         fetch.wait()
-        over(lambda plane: wait_plane(count, plane, recv_f, rf_sem))
-        over(lambda plane: wait_plane(count, plane, send_f, sf_sem))
-        mix_modes(
-            planes, count, recv_f, send_b, wbuf, xf_ref, xi_ref, flat, spec, rows, mixed, turned
-        )
+        over(lambda plane: wait_plane(count - 1, plane, recv_f, rf_sem))
+        over(lambda plane: wait_plane(count - 1, plane, send_f, sf_sem))
+        mix_modes(planes, count, recv_f, wbuf, xf_ref, flat, spec, rows, mixed, turned)
         if layer + 1 < LAYERS:
             fetch = pltpu.make_async_copy(w_hbm.at[layer + 1], wbuf, w_sem.at[layer + 1])
             fetch.start()
@@ -704,12 +749,43 @@
         def turn(index):
             return lax.rem(planes - index, planes) if last else index
 
-        over(lambda n: send_plane(me, count, turn(n), send_b, recv_b, sb_sem, rb_sem))
+        pairs = [(pair, jj) for pair in range(C * MZ // LANES // 2) for jj in range(MY // count)]
+        if last:
+            parts = count - 1
+            for pair, jj in pairs:
+                if jj == 0:
+                    tile = mixed_tile(pair, turned)
+                to_planes(xi_ref[...], tile[jj], jj, pair, count, flat)
+            pack_planes(planes, count, 0, count, flat, send_b)
+            over(lambda n: send_plane(me, count, turn(n), send_b, recv_b, sb_sem, rb_sem))
+        else:
+            near = count // 2
+            parts = 2 * (near - 1)
+            swaps = [
+                swap_tile(me, count, n, own_mixed, other_mixed, om_sem, rm_sem)
+                for n in range(len(pairs))
+            ]
+            for n, (pair, jj) in enumerate(pairs):
+                if jj == 0:
+                    tile = mixed_tile(pair, turned)
+                own_mixed[n] = tile[jj]
+                swaps[n].start()
+            table = xh_ref.at[me // near]
+            for other in range(2):
+                for n, (pair, jj) in enumerate(pairs):
+                    if other:
+                        swaps[n].wait_recv()
+                    tile = other_mixed[n] if other else own_mixed[n]
+                    to_planes(table[...], tile, jj, pair, count, flat)
+                pack_planes(planes, count, other * near, near, flat, send_b)
+                over(lambda n: send_half(me, count, n, other, send_b, recv_b, sb_sem, rb_sem))
+            for swap in swaps:
+                swap.wait_send()
         kp = kp_ref.at[layer]
 
         def rest(index):
             plane = turn(index)
-            wait_plane(count, plane, recv_b, rb_sem)
+            wait_plane(parts, plane, recv_b, rb_sem)
             from_modes(plane, count, recv_b, yi_ref, zi_ref, flat, sp)
             if not last:
                 middle_plane(plane, kp, hid, sp, zs)
@@ -733,7 +809,7 @@
                     add_face(plane, st_ref, res_ref, cond)
 
         over(rest)
-        over(lambda plane: wait_plane(count, plane, send_b, sb_sem))
+        over(lambda plane: wait_plane(parts, plane, send_b, sb_sem))
     add_face(0, st_ref, res_ref, cond)
     for side in range(2):
         edge_copy(me, count, side, edge_send, edge_recv, es_sem, er_sem).wait()
@@ -801,7 +877,7 @@
         point_weight,
         dec_in,
         dec_out.T,
-    ) + tuple(tables[name] for name in ("zf", "zi", "yf", "yi", "xf", "xi"))
+    ) + tuple(tables[name] for name in ("zf", "zi", "yf", "yi", "xf", "xi", "xh"))
     operands = operands + (well_cells, well_rates)
     vmem = pl.BlockSpec(memory_space=pltpu.VMEM)
     exchange = pltpu.VMEM((planes, count, slots, LANES), BF)
@@ -840,10 +916,13 @@
             pltpu.VMEM((NZ, 3 * WELLS), BF),
             pltpu.VMEM((2, 2, NY, NZ), BF),
             pltpu.VMEM((2, 2, NY, NZ), BF),
+            pltpu.VMEM((modes * C // 256, 2 * MX, 256), BF),
+            pltpu.VMEM((modes * C // 256, 2 * MX, 256), BF),
             pltpu.SemaphoreType.DMA((LAYERS,)),
         ]
         + [pltpu.SemaphoreType.DMA((planes,))] * 4
-        + [pltpu.SemaphoreType.DMA((2,))] * 2,
+        + [pltpu.SemaphoreType.DMA((2,))] * 2
+        + [pltpu.SemaphoreType.DMA((modes * C // 256,))] * 2,
         compiler_params=pltpu.CompilerParams(
             collective_id=0, has_side_effects=True, vmem_limit_bytes=60 * 1024 * 1024
         ),

time: 129 us -> 125 us (0.969)
  Pallas kernels: 123 us -> 118 us
    pallas_call x1, Pallas kernels: 123 us -> 118 us  [local_fast(): pl.pallas_call(lambda *refs: whole_kernel(planes, count, *refs), in_specs...]
where the time goes in v5:
time: 125 us; the launch traced here: 123 us
  Pallas kernels  118 us (94%)
  local copies, waits for them, and re-layouts  4.17 us (3%)
    pallas_call x1, Pallas kernels, local_fast(): pl.pallas_call(lambda *refs: whole_kernel(planes, count, *refs), in_specs...  118 us
    unnamed x2, local copies, waits for them, and re-layouts  4.17 us

profile of v5, /device:TPU:1, one launch (start us, length us, event | category | flops | bytes accessed | tf_op | source)
XLA Modules:
  0.0 123.3 jit_solution(12797234709632003195)
XLA Ops:
  0.6 118.4 %whole.1 = (f32[1,2,8,128,128]{4,3,2,1,0:T(8,128)}, f32[1,8,128,128]{3,2,1,0:T(8,128)}) custom-call(bf16[1,4,8,128,128]{4,3,2,1,0:T(8,128)(2,1)} %refs_0_.1, f32[1,8,128,128]{3,2,1,0:T(8,128)} %refs_1_.1, bf16[5,128]{1,0:T(8,128)(2,1)} %refs_2_.1, bf16[32,128]{1,0:T(8,128)(2,1)} %bitcast.2, bf16[2,32,32]{2,1,0:T(8,128)(2,1)} %refs_4_.1, ...), custom_call_target="tpu_custom_call" | custom-call | tf_op jit(solution)/shard_map/whole/pallas_call | solution.py:884
  119.1 2.3 %copy.21 = f32[1,2,8,128,128]{4,3,2,1,0:T(8,128)} copy(f32[1,2,8,128,128]{4,3,2,1,0:T(8,128)} %get-tuple-element.4) | data formatting | bytes 2097152
  121.4 1.9 %copy.22 = f32[1,8,128,128]{3,2,1,0:T(8,128)} copy(f32[1,8,128,128]{3,2,1,0:T(8,128)} %get-tuple-element.5) | data formatting | bytes 1048576

commit v6 on v5

--- a/solution.py
+++ b/solution.py
@@ -881,7 +881,7 @@
     operands = operands + (well_cells, well_rates)
     vmem = pl.BlockSpec(memory_space=pltpu.VMEM)
     exchange = pltpu.VMEM((planes, count, slots, LANES), BF)
-    return pl.pallas_call(
+    results = pl.pallas_call(
         lambda *refs: whole_kernel(planes, count, *refs),
         in_specs=[vmem] * len(operands) + [pl.BlockSpec(memory_space=pl.ANY)],
         out_specs=[vmem, vmem],
@@ -928,6 +928,44 @@
         ),
         name="whole",
     )(*operands, spec_weight)
+    return handed_on(results)
+
+
+def handed_on(results):
+    pieces = [
+        (n, at) for n, each in enumerate(results) for at in np.ndindex(*each.shape[:-2])
+    ]
+
+    def body(*refs):
+        source, target, held = refs[:2], refs[2:4], refs[4:6]
+        in_sem, out_sem = refs[6:]
+        loads = [
+            pltpu.make_async_copy(source[n].at[at], held[n].at[at], in_sem.at[k])
+            for k, (n, at) in enumerate(pieces)
+        ]
+        stores = [
+            pltpu.make_async_copy(held[n].at[at], target[n].at[at], out_sem.at[k])
+            for k, (n, at) in enumerate(pieces)
+        ]
+        for load in loads:
+            load.start()
+        for load, store in zip(loads, stores):
+            load.wait()
+            store.start()
+        for store in stores:
+            store.wait()
+
+    whole = pl.BlockSpec(memory_space=pl.ANY)
+    return pl.pallas_call(
+        body,
+        in_specs=[whole] * 2,
+        out_specs=[whole] * 2,
+        out_shape=[jax.ShapeDtypeStruct(each.shape, each.dtype) for each in results],
+        scratch_shapes=[pltpu.VMEM(each.shape, each.dtype) for each in results]
+        + [pltpu.SemaphoreType.DMA((len(pieces),))] * 2,
+        compiler_params=pltpu.CompilerParams(vmem_limit_bytes=60 * 1024 * 1024),
+        name="handed_on",
+    )(*results)
 
 
 def local(features, log_perm, well_cells, well_rates, lift_in, lift_out, spec_weight, *rest):

time: 125 us -> 123 us (0.984)
  local copies, waits for them, and re-layouts: 4.17 us -> 0 us
  Pallas kernels: 118 us -> 121 us
    unnamed x2 -> x0, local copies, waits for them, and re-layouts: 4.17 us -> none
    pallas_call x0 -> x1, Pallas kernels: none -> 2.47 us  [handed_on(): pl.pallas_call(body, in_specs=[whole] * 2, out_specs=[whole] * 2, out_sha...]
where the time goes in v6:
time: 123 us; the launch traced here: 122 us
  Pallas kernels  121 us (98%)
    pallas_call x1, Pallas kernels, local_fast(): pl.pallas_call(lambda *refs: whole_kernel(planes, count, *refs), in_specs...  118 us
    pallas_call x1, Pallas kernels, handed_on(): pl.pallas_call(body, in_specs=[whole] * 2, out_specs=[whole] * 2, out_sha...  2.47 us

profile of v6, /device:TPU:1, one launch (start us, length us, event | category | flops | bytes accessed | tf_op | source)
XLA Modules:
  0.0 121.6 jit_solution(2446660156651766199)
XLA Ops:
  0.6 118.5 %whole.1 = (f32[1,2,8,128,128]{4,3,2,1,0:T(8,128)}, f32[1,8,128,128]{3,2,1,0:T(8,128)}) custom-call(bf16[1,4,8,128,128]{4,3,2,1,0:T(8,128)(2,1)} %refs_0_.1, f32[1,8,128,128]{3,2,1,0:T(8,128)} %refs_1_.1, bf16[5,128]{1,0:T(8,128)(2,1)} %refs_2_.1, bf16[32,128]{1,0:T(8,128)(2,1)} %bitcast.2, bf16[2,32,32]{2,1,0:T(8,128)(2,1)} %refs_4_.1, ...), custom_call_target="tpu_custom_call" | custom-call | tf_op jit(solution)/shard_map/whole/pallas_call | solution.py:884
  119.1 2.5 %handed_on.1 = (f32[1,2,8,128,128]{4,3,2,1,0:T(8,128)}, f32[1,8,128,128]{3,2,1,0:T(8,128)}) custom-call(f32[1,2,8,128,128]{4,3,2,1,0:T(8,128)} %get-tuple-element.4.refs_0_, f32[1,8,128,128]{3,2,1,0:T(8,128)} %get-tuple-element.5.refs_1_), custom_call_target="tpu_custom_call" | custom-call | tf_op jit(solution)/shard_map/handed_on/pallas_call | solution.py:959

commit v7 on v6

--- a/solution.py
+++ b/solution.py
@@ -217,6 +217,7 @@
 SKEW = 4
 PITCH = PAIRS + SKEW
 MODE_STEP = 8
+SOON = (5, 3)
 ROWS = 8
 LOOK = 4
 LAG = 1
@@ -299,9 +300,39 @@
     recv[plane, me] = send[plane, me]
 
 
+def mode_half(jj, count):
+    span = 2 * C * MZ // LANES
+    return pl.ds(jj * span, span)
+
+
+def send_modes(me, count, plane, jj, send, recv, send_sem, recv_sem):
+    part = mode_half(jj, count)
+    for shift in range(1, count):
+        target = lax.rem(me + shift, count)
+        pltpu.make_async_remote_copy(
+            src_ref=send.at[plane, target, part],
+            dst_ref=recv.at[plane, me, part],
+            send_sem=send_sem.at[plane, jj],
+            recv_sem=recv_sem.at[plane, jj],
+            device_id={"space": target},
+            device_id_type=pl.DeviceIdType.MESH,
+        ).start()
+    recv[plane, me, part] = send[plane, me, part]
+
+
+def wait_modes(count, plane, jj, buffer, sem):
+    part = buffer.at[plane, pl.ds(0, count - 1), mode_half(jj, count)]
+    pltpu.make_async_copy(part, part, sem.at[plane, jj]).wait()
+
+
 def wait_plane(parts, plane, buffer, sem):
     part = buffer.at[plane, pl.ds(0, parts)]
     pltpu.make_async_copy(part, part, sem.at[plane]).wait()
+
+
+def slot_of(s, count):
+    own = MY // count
+    return (s % own * 2 + s // own) * (C * MZ // LANES)
 
 
 def to_modes(plane, count, zf_ref, yf_ref, zs, flat, send):
@@ -329,7 +360,8 @@
         modes = dot32(yf_ref[...], jnp.concatenate(columns, 1))
         for s in range(2 * MY // count):
             for half in range(2):
-                flat[pl.ds(s * tiles + pair * 2 + half, count, stride=slots + SKEW), :] = modes[
+                slot = slot_of(s, count) + pair * 2 + half
+                flat[pl.ds(slot, count, stride=slots + SKEW), :] = modes[
                     s * count : (s + 1) * count, half * LANES : (half + 1) * LANES
                 ]
     for dst in range(count):
@@ -392,7 +424,7 @@
         rows = []
         for s in range(2 * MY // count):
             part = [
-                flat[pl.ds(s * tiles + pair * 2 + half, count, stride=slots + SKEW), :]
+                flat[pl.ds(slot_of(s, count) + pair * 2 + half, count, stride=slots + SKEW), :]
                 for half in range(2)
             ]
             rows.append(jnp.concatenate(part, 1))
@@ -534,7 +566,7 @@
     ends[...] = jnp.where((cells[...] & (NZ - 1)) == column, 1.0, 0.0).astype(BF)
 
 
-def mix_modes(planes, count, recv, wbuf, xf_ref, flat, spec, rows, mixed, turned):
+def mix_modes(planes, count, jj, recv, wbuf, xf_ref, flat, spec, rows, mixed, turned):
     own = MY // count
     tiles = C * MZ // LANES
     slots = 2 * own * tiles
@@ -546,16 +578,16 @@
 
     def unpack(plane, carry):
         for src in range(count):
-            start = (plane * count + src) * pitch
-            flat[pl.ds(start, slots), :] = recv[plane, src].astype(F32)
+            start = (plane * count + src) * pitch + jj * 2 * tiles
+            flat[pl.ds(start, 2 * tiles), :] = recv[plane, src, mode_half(jj, count)].astype(F32)
         return carry
 
     lax.fori_loop(0, planes, unpack, 0)
 
     def column(p, t):
-        return flat[pl.ds(p * own * tiles + t, every, stride=pitch), :].astype(BF)
-
-    for pair in range(own * tiles // 2):
+        return flat[pl.ds((jj * 2 + p) * tiles + t, every, stride=pitch), :].astype(BF)
+
+    for pair in range(tiles // 2):
         right = jnp.concatenate(
             [
                 jnp.concatenate([column(p, pair * 2 + half) for half in range(2)], 1)
@@ -569,10 +601,9 @@
             for r in range(4):
                 first = (pair * 2 + half) * 4 + r
                 spec[pl.ds(first * (MZ + SKEW), MZ), : 2 * MX] = part[r * MZ : (r + 1) * MZ, :]
-    groups = own * MZ // MODE_STEP
+    groups = MZ // MODE_STEP
     for group in range(groups):
-        jj, k = group * MODE_STEP // MZ, group * MODE_STEP % MZ
-        base = jj * C * (MZ + SKEW) + k
+        base = group * MODE_STEP
         picked = [
             spec[pl.ds(base + r, C, stride=MZ + SKEW), : 2 * MX] for r in range(MODE_STEP)
         ]
@@ -585,6 +616,7 @@
 
     def step(group, carry):
         first = pl.multiple_of(group * MODE_STEP, MODE_STEP)
+        wfirst = pl.multiple_of(jj * MZ + group * MODE_STEP, MODE_STEP)
         for piece in range(MX // per):
             left = []
             for i in range(per):
@@ -592,7 +624,7 @@
                     row = rows[group, pl.ds(q * MX + piece * per + i, MODE_STEP, stride=0), :]
                     left.append(jnp.where(own_mode, row, 0.0))
             lo = piece * wide
-            weights = wbuf[pl.ds(first, MODE_STEP), :, lo : lo + wide].reshape(wide, wide)
+            weights = wbuf[pl.ds(wfirst, MODE_STEP), :, lo : lo + wide].reshape(wide, wide)
             both = dot32(jnp.concatenate(left, 0).astype(BF), weights)
 
             def part(i, q, t):
@@ -612,22 +644,21 @@
         part = mixed[:, block * LANES : (block + 1) * LANES].T
         for r in range(4):
             first = (block * 4 + r) * (C + SKEW)
-            turned[pl.ds(first, C), : own * MZ] = part[r * C : (r + 1) * C, :]
+            turned[pl.ds(first, C), :MZ] = part[r * C : (r + 1) * C, :]
 
 
 def mixed_tile(pair, turned):
     lane = lax.broadcasted_iota(jnp.int32, (1, LANES), 1)
     low = lane < 64
     even = lane % 64 < 32
-    right = [[], []]
+    right = []
     for half in range(2):
         o = (pair * 2 + half) * 4
         a = [turned[pl.ds(o + r, 2 * MX, stride=C + SKEW), :] for r in range(4)]
         b = jnp.where(low, a[0], pltpu.roll(a[2], 64, 1))
         c = jnp.where(low, a[1], pltpu.roll(a[3], 64, 1))
-        right[0].append(jnp.where(even, b, pltpu.roll(c, 32, 1)))
-        right[1].append(jnp.where(even, pltpu.roll(b, LANES - 32, 1), c))
-    return [jnp.concatenate(part, 1).astype(BF) for part in right]
+        right.append(jnp.where(even, b, pltpu.roll(c, 32, 1)))
+    return jnp.concatenate(right, 1).astype(BF)
 
 
 def to_planes(table, tile, jj, pair, count, flat):
@@ -638,7 +669,7 @@
     every = back.shape[0] // 2
     for p in range(2):
         for half in range(2):
-            slot = (p * own + jj) * tiles + pair * 2 + half
+            slot = (jj * 2 + p) * tiles + pair * 2 + half
             flat[pl.ds(slot, every, stride=pitch), :] = back[
                 p * every : (p + 1) * every, half * LANES : (half + 1) * LANES
             ]
@@ -730,53 +761,71 @@
 
         lax.fori_loop(0, planes, run, 0)
 
+    own = MY // count
+
+    def send_forward(plane, soon):
+        send_modes(me, count, plane, 0, send_f, recv_f, sf_sem, rf_sem)
+
+        @pl.when(plane < soon)
+        def _():
+            send_rest(plane)
+
+    def send_rest(plane):
+        for jj in range(1, own):
+            send_modes(me, count, plane, jj, send_f, recv_f, sf_sem, rf_sem)
+
+    def send_late(soon):
+        lax.fori_loop(soon, planes, lambda plane, carry: (send_rest(plane), carry)[1], 0)
+
     def lift(plane):
         lift_plane(plane, feat_ref, perm_ref, in_ref, lo_ref, hid, plain, xs, zs)
         to_modes(plane, count, zf_ref, yf_ref, zs, flat, send_f)
-        send_plane(me, count, plane, send_f, recv_f, sf_sem, rf_sem)
+        send_forward(plane, SOON[0])
 
     over(lift)
+    send_late(SOON[0])
     for layer in range(LAYERS):
         fetch.wait()
-        over(lambda plane: wait_plane(count - 1, plane, recv_f, rf_sem))
-        over(lambda plane: wait_plane(count - 1, plane, send_f, sf_sem))
-        mix_modes(planes, count, recv_f, wbuf, xf_ref, flat, spec, rows, mixed, turned)
-        if layer + 1 < LAYERS:
+        last = layer + 1 == LAYERS
+        tile_pairs = C * MZ // LANES // 2
+        swaps = [
+            swap_tile(me, count, n, own_mixed, other_mixed, om_sem, rm_sem)
+            for n in range(0 if last else own * tile_pairs)
+        ]
+        for jj in range(own):
+            over(lambda plane: wait_modes(count, plane, jj, recv_f, rf_sem))
+            mix_modes(planes, count, jj, recv_f, wbuf, xf_ref, flat, spec, rows, mixed, turned)
+            for pair in range(tile_pairs):
+                tile = mixed_tile(pair, turned)
+                if last:
+                    to_planes(xi_ref[...], tile, jj, pair, count, flat)
+                else:
+                    n = jj * tile_pairs + pair
+                    own_mixed[n] = tile
+                    swaps[n].start()
+        for jj in range(own):
+            over(lambda plane: wait_modes(count, plane, jj, send_f, sf_sem))
+        if not last:
             fetch = pltpu.make_async_copy(w_hbm.at[layer + 1], wbuf, w_sem.at[layer + 1])
             fetch.start()
-        last = layer + 1 == LAYERS
 
         def turn(index):
             return lax.rem(planes - index, planes) if last else index
 
-        pairs = [(pair, jj) for pair in range(C * MZ // LANES // 2) for jj in range(MY // count)]
         if last:
             parts = count - 1
-            for pair, jj in pairs:
-                if jj == 0:
-                    tile = mixed_tile(pair, turned)
-                to_planes(xi_ref[...], tile[jj], jj, pair, count, flat)
             pack_planes(planes, count, 0, count, flat, send_b)
             over(lambda n: send_plane(me, count, turn(n), send_b, recv_b, sb_sem, rb_sem))
         else:
             near = count // 2
             parts = 2 * (near - 1)
-            swaps = [
-                swap_tile(me, count, n, own_mixed, other_mixed, om_sem, rm_sem)
-                for n in range(len(pairs))
-            ]
-            for n, (pair, jj) in enumerate(pairs):
-                if jj == 0:
-                    tile = mixed_tile(pair, turned)
-                own_mixed[n] = tile[jj]
-                swaps[n].start()
             table = xh_ref.at[me // near]
             for other in range(2):
-                for n, (pair, jj) in enumerate(pairs):
+                for n, swap in enumerate(swaps):
                     if other:
-                        swaps[n].wait_recv()
+                        swap.wait_recv()
                     tile = other_mixed[n] if other else own_mixed[n]
-                    to_planes(table[...], tile, jj, pair, count, flat)
+                    to_planes(table[...], tile, n // tile_pairs, n % tile_pairs, count, flat)
                 pack_planes(planes, count, other * near, near, flat, send_b)
                 over(lambda n: send_half(me, count, n, other, send_b, recv_b, sb_sem, rb_sem))
             for swap in swaps:
@@ -790,7 +839,7 @@
             if not last:
                 middle_plane(plane, kp, hid, sp, zs)
                 to_modes(plane, count, zf_ref, yf_ref, zs, flat, send_f)
-                send_plane(me, count, plane, send_f, recv_f, sf_sem, rf_sem)
+                send_forward(plane, SOON[1])
             else:
                 final_plane(plane, kp, di_ref, do_ref, perm_ref, hid, sp, st_ref)
                 residual_plane(
@@ -809,6 +858,8 @@
                     add_face(plane, st_ref, res_ref, cond)
 
         over(rest)
+        if not last:
+            send_late(SOON[1])
         over(lambda plane: wait_plane(parts, plane, send_b, sb_sem))
     add_face(0, st_ref, res_ref, cond)
     for side in range(2):
@@ -897,9 +948,9 @@
             exchange,
             exchange,
             pltpu.VMEM((planes * count * (slots + SKEW), LANES), F32),
-            pltpu.VMEM((own * C * (MZ + SKEW), LANES), F32),
-            pltpu.VMEM((modes // MODE_STEP, 2 * MX, MODE_STEP * C), F32),
-            pltpu.VMEM((modes, MX * 2 * C), F32),
+            pltpu.VMEM((C * (MZ + SKEW), LANES), F32),
+            pltpu.VMEM((MZ // MODE_STEP, 2 * MX, MODE_STEP * C), F32),
+            pltpu.VMEM((MZ, MX * 2 * C), F32),
             pltpu.VMEM((2 * MX * (C + SKEW), LANES), F32),
             pltpu.VMEM((2, C * PITCH, LANES), F32),
             pltpu.VMEM((2, PAIRS * (C + SKEW), LANES), F32),
@@ -920,7 +971,8 @@
             pltpu.VMEM((modes * C // 256, 2 * MX, 256), BF),
             pltpu.SemaphoreType.DMA((LAYERS,)),
         ]
-        + [pltpu.SemaphoreType.DMA((planes,))] * 4
+        + [pltpu.SemaphoreType.DMA((planes, own))] * 2
+        + [pltpu.SemaphoreType.DMA((planes,))] * 2
         + [pltpu.SemaphoreType.DMA((2,))] * 2
         + [pltpu.SemaphoreType.DMA((modes * C // 256,))] * 2,
         compiler_params=pltpu.CompilerParams(

time: 123 us -> 118 us (0.959)
  Pallas kernels: 121 us -> 117 us
    pallas_call x1, Pallas kernels: 118 us -> 115 us  [local_fast(): pl.pallas_call(lambda *refs: whole_kernel(planes, count, *refs), in_specs...]
where the time goes in v7:
time: 118 us
  Pallas kernels  117 us (99%)
    pallas_call x1, Pallas kernels, local_fast(): pl.pallas_call(lambda *refs: whole_kernel(planes, count, *refs), in_specs...  115 us
    pallas_call x1, Pallas kernels, handed_on(): pl.pallas_call(body, in_specs=[whole] * 2, out_specs=[whole] * 2, out_sha...  2.47 us

profile of v7, /device:TPU:1, one launch (start us, length us, event | category | flops | bytes accessed | tf_op | source)
XLA Modules:
  0.0 117.7 jit_solution(5252648866371886842)
XLA Ops:
  0.6 114.6 %whole.1 = (f32[1,2,8,128,128]{4,3,2,1,0:T(8,128)}, f32[1,8,128,128]{3,2,1,0:T(8,128)}) custom-call(bf16[1,4,8,128,128]{4,3,2,1,0:T(8,128)(2,1)} %refs_0_.1, f32[1,8,128,128]{3,2,1,0:T(8,128)} %refs_1_.1, bf16[5,128]{1,0:T(8,128)(2,1)} %refs_2_.1, bf16[32,128]{1,0:T(8,128)(2,1)} %bitcast.2, bf16[2,32,32]{2,1,0:T(8,128)(2,1)} %refs_4_.1, ...), custom_call_target="tpu_custom_call" | custom-call | tf_op jit(solution)/shard_map/whole/pallas_call | solution.py:935
  115.3 2.5 %handed_on.1 = (f32[1,2,8,128,128]{4,3,2,1,0:T(8,128)}, f32[1,8,128,128]{3,2,1,0:T(8,128)}) custom-call(f32[1,2,8,128,128]{4,3,2,1,0:T(8,128)} %get-tuple-element.4.refs_0_, f32[1,8,128,128]{3,2,1,0:T(8,128)} %get-tuple-element.5.refs_1_), custom_call_target="tpu_custom_call" | custom-call | tf_op jit(solution)/shard_map/handed_on/pallas_call | solution.py:1011

commit v8 on v7

--- a/solution.py
+++ b/solution.py
@@ -218,6 +218,7 @@
 PITCH = PAIRS + SKEW
 MODE_STEP = 8
 SOON = (5, 3)
+EARLY = 3
 ROWS = 8
 LOOK = 4
 LAG = 1
@@ -286,29 +287,18 @@
     return u + u * jnp.tanh(inner)
 
 
-def send_plane(me, count, plane, send, recv, send_sem, recv_sem):
-    for shift in range(1, count):
-        target = lax.rem(me + shift, count)
-        pltpu.make_async_remote_copy(
-            src_ref=send.at[plane, target],
-            dst_ref=recv.at[plane, me],
-            send_sem=send_sem.at[plane],
-            recv_sem=recv_sem.at[plane],
-            device_id={"space": target},
-            device_id_type=pl.DeviceIdType.MESH,
-        ).start()
-    recv[plane, me] = send[plane, me]
-
-
 def mode_half(jj, count):
     span = 2 * C * MZ // LANES
     return pl.ds(jj * span, span)
 
 
+def others(me, count):
+    return [lax.rem(me + shift, count) for shift in range(1, count)]
+
+
 def send_modes(me, count, plane, jj, send, recv, send_sem, recv_sem):
     part = mode_half(jj, count)
-    for shift in range(1, count):
-        target = lax.rem(me + shift, count)
+    for target in others(me, count):
         pltpu.make_async_remote_copy(
             src_ref=send.at[plane, target, part],
             dst_ref=recv.at[plane, me, part],
@@ -327,7 +317,7 @@
 
 def wait_plane(parts, plane, buffer, sem):
     part = buffer.at[plane, pl.ds(0, parts)]
-    pltpu.make_async_copy(part, part, sem.at[plane]).wait()
+    pltpu.make_async_copy(part, part, sem.at[plane, 0]).wait()
 
 
 def slot_of(s, count):
@@ -675,14 +665,16 @@
             ]
 
 
-def pack_planes(planes, count, first, targets, flat, send):
+def pack_planes(planes, count, first, targets, some, flat, send):
     slots = 2 * MY // count * C * MZ // LANES
-    pitch = slots + SKEW
 
     def pack(plane, carry):
         for dst in range(targets):
-            start = (plane * targets + dst) * pitch
-            send[plane, first + dst] = flat[pl.ds(start, slots), :].astype(BF)
+            start = (plane * targets + dst) * (slots + SKEW)
+            for jj in some:
+                part = mode_half(jj, count)
+                rows = flat[pl.ds(start + part.start, part.size), :]
+                send[plane, first + dst, part] = rows.astype(BF)
         return carry
 
     lax.fori_loop(0, planes, pack, 0)
@@ -696,8 +688,8 @@
         pltpu.make_async_remote_copy(
             src_ref=send.at[plane, other * near + place],
             dst_ref=recv.at[plane, owner],
-            send_sem=send_sem.at[plane],
-            recv_sem=recv_sem.at[plane],
+            send_sem=send_sem.at[plane, 0],
+            recv_sem=recv_sem.at[plane, 0],
             device_id={"space": me // near * near + place},
             device_id_type=pl.DeviceIdType.MESH,
         ).start()
@@ -788,6 +780,29 @@
         fetch.wait()
         last = layer + 1 == LAYERS
         tile_pairs = C * MZ // LANES // 2
+
+        def turn(index):
+            return lax.rem(planes - index, planes) if last else index
+
+        def send_back(jj):
+            def one(n, carry):
+                if jj > 0:
+
+                    @pl.when(n >= EARLY)
+                    def _():
+                        for before in range(jj):
+                            send_modes(me, count, turn(n), before, send_b, recv_b, sb_sem, rb_sem)
+
+                if jj + 1 == own:
+                    send_modes(me, count, turn(n), jj, send_b, recv_b, sb_sem, rb_sem)
+                return carry
+
+            if jj + 1 < own:
+                for n in range(EARLY):
+                    send_modes(me, count, (planes - n) % planes, jj, send_b, recv_b, sb_sem, rb_sem)
+            else:
+                lax.fori_loop(0, planes, one, 0)
+
         swaps = [
             swap_tile(me, count, n, own_mixed, other_mixed, om_sem, rm_sem)
             for n in range(0 if last else own * tile_pairs)
@@ -803,20 +818,16 @@
                     n = jj * tile_pairs + pair
                     own_mixed[n] = tile
                     swaps[n].start()
+            if last:
+                pack_planes(planes, count, 0, count, (jj,), flat, send_b)
+                send_back(jj)
         for jj in range(own):
             over(lambda plane: wait_modes(count, plane, jj, send_f, sf_sem))
         if not last:
             fetch = pltpu.make_async_copy(w_hbm.at[layer + 1], wbuf, w_sem.at[layer + 1])
             fetch.start()
 
-        def turn(index):
-            return lax.rem(planes - index, planes) if last else index
-
-        if last:
-            parts = count - 1
-            pack_planes(planes, count, 0, count, flat, send_b)
-            over(lambda n: send_plane(me, count, turn(n), send_b, recv_b, sb_sem, rb_sem))
-        else:
+        if not last:
             near = count // 2
             parts = 2 * (near - 1)
             table = xh_ref.at[me // near]
@@ -826,15 +837,22 @@
                         swap.wait_recv()
                     tile = other_mixed[n] if other else own_mixed[n]
                     to_planes(table[...], tile, n // tile_pairs, n % tile_pairs, count, flat)
-                pack_planes(planes, count, other * near, near, flat, send_b)
+                pack_planes(planes, count, other * near, near, range(own), flat, send_b)
                 over(lambda n: send_half(me, count, n, other, send_b, recv_b, sb_sem, rb_sem))
             for swap in swaps:
                 swap.wait_send()
         kp = kp_ref.at[layer]
 
+        def settle(plane, buffer, sem):
+            if not last:
+                wait_plane(parts, plane, buffer, sem)
+            for jj in range(own if last else 0):
+                wait_modes(count, plane, jj, buffer, sem)
+
+
         def rest(index):
             plane = turn(index)
-            wait_plane(parts, plane, recv_b, rb_sem)
+            settle(plane, recv_b, rb_sem)
             from_modes(plane, count, recv_b, yi_ref, zi_ref, flat, sp)
             if not last:
                 middle_plane(plane, kp, hid, sp, zs)
@@ -860,7 +878,7 @@
         over(rest)
         if not last:
             send_late(SOON[1])
-        over(lambda plane: wait_plane(parts, plane, send_b, sb_sem))
+        over(lambda plane: settle(plane, send_b, sb_sem))
     add_face(0, st_ref, res_ref, cond)
     for side in range(2):
         edge_copy(me, count, side, edge_send, edge_recv, es_sem, er_sem).wait()
@@ -971,8 +989,7 @@
             pltpu.VMEM((modes * C // 256, 2 * MX, 256), BF),
             pltpu.SemaphoreType.DMA((LAYERS,)),
         ]
-        + [pltpu.SemaphoreType.DMA((planes, own))] * 2
-        + [pltpu.SemaphoreType.DMA((planes,))] * 2
+        + [pltpu.SemaphoreType.DMA((planes, own))] * 4
         + [pltpu.SemaphoreType.DMA((2,))] * 2
         + [pltpu.SemaphoreType.DMA((modes * C // 256,))] * 2,
         compiler_params=pltpu.CompilerParams(

time: 118 us -> 114 us (0.966)
  Pallas kernels: 117 us -> 113 us
    pallas_call x1, Pallas kernels: 115 us -> 110 us  [local_fast(): pl.pallas_call(lambda *refs: whole_kernel(planes, count, *refs), in_specs...]
where the time goes in v8:
time: 114 us; the launch traced here: 113 us
  Pallas kernels  113 us (99%)
    pallas_call x1, Pallas kernels, local_fast(): pl.pallas_call(lambda *refs: whole_kernel(planes, count, *refs), in_specs...  110 us
    pallas_call x1, Pallas kernels, handed_on(): pl.pallas_call(body, in_specs=[whole] * 2, out_specs=[whole] * 2, out_sha...  2.47 us

profile of v8, /device:TPU:1, one launch (start us, length us, event | category | flops | bytes accessed | tf_op | source)
XLA Modules:
  0.0 113.2 jit_solution(14643710692125034937)
XLA Ops:
  0.6 110.1 %whole.1 = (f32[1,2,8,128,128]{4,3,2,1,0:T(8,128)}, f32[1,8,128,128]{3,2,1,0:T(8,128)}) custom-call(bf16[1,4,8,128,128]{4,3,2,1,0:T(8,128)(2,1)} %refs_0_.1, f32[1,8,128,128]{3,2,1,0:T(8,128)} %refs_1_.1, bf16[5,128]{1,0:T(8,128)(2,1)} %refs_2_.1, bf16[32,128]{1,0:T(8,128)(2,1)} %bitcast.2, bf16[2,32,32]{2,1,0:T(8,128)(2,1)} %refs_4_.1, ...), custom_call_target="tpu_custom_call" | custom-call | tf_op jit(solution)/shard_map/whole/pallas_call | solution.py:953
  110.7 2.5 %handed_on.1 = (f32[1,2,8,128,128]{4,3,2,1,0:T(8,128)}, f32[1,8,128,128]{3,2,1,0:T(8,128)}) custom-call(f32[1,2,8,128,128]{4,3,2,1,0:T(8,128)} %get-tuple-element.4.refs_0_, f32[1,8,128,128]{3,2,1,0:T(8,128)} %get-tuple-element.5.refs_1_), custom_call_target="tpu_custom_call" | custom-call | tf_op jit(solution)/shard_map/handed_on/pallas_call | solution.py:1028

commit v9 on v8

--- a/solution.py
+++ b/solution.py
@@ -597,7 +597,7 @@
         picked = [
             spec[pl.ds(base + r, C, stride=MZ + SKEW), : 2 * MX] for r in range(MODE_STEP)
         ]
-        rows[group] = jnp.concatenate(picked, 0).T
+        rows[group, : 2 * MX, :] = jnp.concatenate(picked, 0).T
     wide = MODE_STEP * C
     own_mode = lax.broadcasted_iota(jnp.int32, (MODE_STEP, wide), 0) == (
         lax.broadcasted_iota(jnp.int32, (MODE_STEP, wide), 1) // C
@@ -967,7 +967,7 @@
             exchange,
             pltpu.VMEM((planes * count * (slots + SKEW), LANES), F32),
             pltpu.VMEM((C * (MZ + SKEW), LANES), F32),
-            pltpu.VMEM((MZ // MODE_STEP, 2 * MX, MODE_STEP * C), F32),
+            pltpu.VMEM((MZ // MODE_STEP, 2 * MX + MODE_STEP, MODE_STEP * C), F32),
             pltpu.VMEM((MZ, MX * 2 * C), F32),
             pltpu.VMEM((2 * MX * (C + SKEW), LANES), F32),
             pltpu.VMEM((2, C * PITCH, LANES), F32),

time: 114 us -> 114 us (level)
  no operation moved by 1% of the time
where the time goes in v9:
time: 114 us; the launch traced here: 113 us
  Pallas kernels  112 us (98%)
    pallas_call x1, Pallas kernels, local_fast(): pl.pallas_call(lambda *refs: whole_kernel(planes, count, *refs), in_specs...  110 us
    pallas_call x1, Pallas kernels, handed_on(): pl.pallas_call(body, in_specs=[whole] * 2, out_specs=[whole] * 2, out_sha...  2.47 us

profile of v9, /device:TPU:1, one launch (start us, length us, event | category | flops | bytes accessed | tf_op | source)
XLA Modules:
  0.0 113.1 jit_solution(16971913949400843664)
XLA Ops:
  0.6 110.0 %whole.1 = (f32[1,2,8,128,128]{4,3,2,1,0:T(8,128)}, f32[1,8,128,128]{3,2,1,0:T(8,128)}) custom-call(bf16[1,4,8,128,128]{4,3,2,1,0:T(8,128)(2,1)} %refs_0_.1, f32[1,8,128,128]{3,2,1,0:T(8,128)} %refs_1_.1, bf16[5,128]{1,0:T(8,128)(2,1)} %refs_2_.1, bf16[32,128]{1,0:T(8,128)(2,1)} %bitcast.2, bf16[2,32,32]{2,1,0:T(8,128)(2,1)} %refs_4_.1, ...), custom_call_target="tpu_custom_call" | custom-call | tf_op jit(solution)/shard_map/whole/pallas_call | solution.py:953
  110.7 2.5 %handed_on.1 = (f32[1,2,8,128,128]{4,3,2,1,0:T(8,128)}, f32[1,8,128,128]{3,2,1,0:T(8,128)}) custom-call(f32[1,2,8,128,128]{4,3,2,1,0:T(8,128)} %get-tuple-element.4.refs_0_, f32[1,8,128,128]{3,2,1,0:T(8,128)} %get-tuple-element.5.refs_1_), custom_call_target="tpu_custom_call" | custom-call | tf_op jit(solution)/shard_map/handed_on/pallas_call | solution.py:1028
